TPU v7x, 256 devices: a whole 4x4x8 slice. The times are simulated.
256 devices in a mesh: pair: 2 (over core), lat: 8 (over y, x_hi), lon: 16 (over z, x_lo).
Axes of the slice: x: 4 (x_hi: 2, x_lo: 2; x = x_hi * 2 + x_lo), y: 4, z: 8, core: 2. Of those that a mesh axis runs over, the one named last changes fastest.
Arguments:
- wave_states: bfloat16 [8, 4, 1536, 7168], P('pair', None, 'lat', 'lon'), may hold values from -6 to 6
- pair_list: int32 [8, 2], replicated, may hold values from 0 to 255
- pair_counts: int32 [2], replicated, may hold values from 0 to 4, as said below
- residuals: float32 [8, 4], replicated, may hold values from -6 to 6
- station_cell: int32 [256], replicated, may hold values from 0 to 11010047
- source_wavelet: float32 [4], replicated, may hold values from -6 to 6
- lat_faces: float32 [1536, 7168], P('lat', 'lon'), may hold values from 0.05 to 0.25
- lon_faces: float32 [1536, 7168], P('lat', 'lon'), may hold values from 0.05 to 0.25
Outputs:
- power_kernel: float32 [1536, 7168], P('lat', 'lon')
Inputs may be any that keep to these rules, and one draw needn't show every extreme that they name: `pair_counts`: slots at and beyond an index's count are unused. One index of pair holds 4 live slots in every draw.
All inputs are finite; a program needn't handle non-finite values.
Results may differ from a plain program's by a relative error of at most 0.0003.
Values may be sent and summed in bfloat16 or wider, within the bound.
A program may use at most 64 MiB of HBM per device.

v0:
```python
import jax
import jax.numpy as jnp
from jax import lax
from jax.sharding import PartitionSpec as P


def extended(block, sides, width, periodic):
    for axis, dim in sides:
        count = lax.axis_size(axis)
        forward = [(i, i + 1) for i in range(count - 1)]
        if periodic:
            forward.append((count - 1, 0))
        backward = [(target, source) for source, target in forward]
        low = lax.ppermute(
            lax.slice_in_dim(block, block.shape[dim] - width, None, axis=dim), axis, forward
        )
        high = lax.ppermute(lax.slice_in_dim(block, 0, width, axis=dim), axis, backward)
        block = jnp.concatenate([low, block, high], axis=dim)
    return block


def copy_for_each(x, axis):
    devices = lax.axis_size(axis)
    return lax.all_to_all(jnp.broadcast_to(x[None], (devices, *x.shape)), axis, 0, 0, tiled=True)


def over_copies(x, axis):
    return copy_for_each(x, axis).sum(axis=0)


def extend(field, width):
    widened = extended(field, (("lon", 3),), width, True)
    return extended(widened, (("lat", 2),), width, False)


def advance(padded, earlier, coef_tile, source):
    centre = padded[:, :, 1:-1, 1:-1]
    north = coef_tile[0, 1:-1, 1:-1]
    above = coef_tile[0, :-2, 1:-1]
    east_face = coef_tile[1, 1:-1, 1:-1]
    west_face = coef_tile[1, 1:-1, :-2]
    change = north * (padded[:, :, 2:, 1:-1] - centre) + above * (padded[:, :, :-2, 1:-1] - centre)
    change = (
        change
        + east_face * (padded[:, :, 1:-1, 2:] - centre)
        + west_face * (padded[:, :, 1:-1, :-2] - centre)
    )
    return 2.0 * centre - earlier + change + source


def point_sources(station_cells, amplitudes, row_first, col_first, height, breadth, nlon):
    row_place = station_cells // nlon - row_first
    col_place = jnp.mod(station_cells % nlon - col_first, nlon)
    row_hit = (lax.broadcasted_iota(jnp.int32, (1, 1, height), 2) == row_place[:, :, None]).astype(
        jnp.float32
    )
    col_hit = (lax.broadcasted_iota(jnp.int32, (1, 1, breadth), 2) == col_place[:, :, None]).astype(
        jnp.float32
    )
    return amplitudes[:, :, None, None] * row_hit[:, :, :, None] * col_hit[:, :, None, :]


def propagate(
    fields,
    station_cells,
    residual_rows,
    active,
    source_wavelet,
    coef_ext,
    row_first,
    col_first,
    nlon,
):
    steps_total = source_wavelet.shape[0]
    height = fields.shape[2]
    breadth = fields.shape[3]
    earlier = fields[:, 0:2]
    current = fields[:, 2:4]
    coef_tile = coef_ext[:, 1:-1, 1:-1]
    summed = jnp.zeros((height, breadth), jnp.float32)

    def amplitudes(moment):
        forward_amp = jnp.broadcast_to(source_wavelet[moment], active.shape)
        return jnp.stack([forward_amp, residual_rows[:, steps_total - 1 - moment]], axis=1)

    for moment in range(0, steps_total, 2):
        padded = extend(jnp.concatenate([earlier, current], axis=1), 2)
        source = point_sources(
            station_cells,
            amplitudes(moment),
            row_first - 1,
            col_first - 1,
            height + 2,
            breadth + 2,
            nlon,
        )
        middle = advance(padded[:, 2:4], padded[:, 0:2, 1:-1, 1:-1], coef_ext, source)
        source = point_sources(
            station_cells, amplitudes(moment + 1), row_first, col_first, height, breadth, nlon
        )
        following = advance(middle, current, coef_tile, source)
        interior = middle[:, :, 1:-1, 1:-1]
        summed = summed + jnp.sum(active[:, None, None] * interior[:, 0] * interior[:, 1], axis=0)
        summed = summed + jnp.sum(active[:, None, None] * following[:, 0] * following[:, 1], axis=0)
        earlier, current = (interior, following)
    return summed


def body(
    wave_states,
    pair_list,
    pair_counts,
    residuals,
    station_cell,
    source_wavelet,
    lat_faces,
    lon_faces,
):
    slot_count = wave_states.shape[0]
    height, breadth = lat_faces.shape
    nlat = height * lax.axis_size("lat")
    nlon = breadth * lax.axis_size("lon")
    row_first = lax.axis_index("lat") * height
    col_first = lax.axis_index("lon") * breadth
    member = lax.axis_index("pair")
    global_rows = row_first + lax.broadcasted_iota(jnp.int32, (height, breadth), 0)
    north = jnp.where(global_rows == nlat - 1, jnp.zeros_like(lat_faces), lat_faces)
    coef_ext = extend(jnp.stack([north, lon_faces])[None], 2)[0]
    cells_all = station_cell[pair_list]
    active = (jnp.arange(slot_count, dtype=jnp.int32) < pair_counts[member]).astype(jnp.float32)
    kernel = propagate(
        wave_states.astype(jnp.float32),
        lax.dynamic_slice_in_dim(cells_all, member * slot_count, slot_count, 0),
        lax.dynamic_slice_in_dim(residuals, member * slot_count, slot_count, 0),
        active,
        source_wavelet,
        coef_ext,
        row_first,
        col_first,
        nlon,
    )
    return over_copies(kernel, "pair")


def solution(mesh):
    in_specs = (
        P("pair", None, "lat", "lon"),
        P(),
        P(),
        P(),
        P(),
        P(),
        P("lat", "lon"),
        P("lat", "lon"),
    )
    out_specs = P("lat", "lon")
    return jax.shard_map(body, mesh=mesh, in_specs=in_specs, out_specs=out_specs, check_vma=False)
```

profile of v0, /device:TPU:1, one launch (start us, length us, event | category | flops | bytes accessed | tf_op | source)
XLA Modules:
  0.0 132.4 jit_solution(9619089637804788533)
XLA Ops:
  0.0 1.2 select_bitcast_fusion
  1.3 1.1 maximum_bitcast_fusion.1
  2.5 2.1 %collective-permute-start.4 = (f32[1,2,192,2]{3,2,1,0:T(8,128)S(1)}, f32[1,2,192,2]{3,2,1,0:T(8,128)S(1)}, u32[]{:S(2)}, u32[]{:S(2)}) collective-permute-start(f32[1,2,192,2]{3,2,1,0:T(8,128)S(1)} %get-tuple-element.31), channel_id=1, source_target_pairs={{0,1},{1,2},{2,3},{3,4},{4,5},{5,6},{6,7},{7,8},{8,9},{9,10},{10,1... | collective-permute-start | bytes 9224 | tf_op jit(solution)/shard_map/ppermute | solution.py:14
  4.6 5.4 %collective-permute-start.5 = (f32[1,2,192,2]{3,2,1,0:T(8,128)S(1)}, f32[1,2,192,2]{3,2,1,0:T(8,128)S(1)}, u32[]{:S(2)}, u32[]{:S(2)}) collective-permute-start(f32[1,2,192,2]{3,2,1,0:T(8,128)S(1)} %get-tuple-element.32), channel_id=1, source_target_pairs={{1,0},{2,1},{3,2},{4,3},{5,4},{6,5},{7,6},{8,7},{9,8},{10,9},{11,1... | collective-permute-start | bytes 9224 | tf_op jit(solution)/shard_map/ppermute | solution.py:17
  10.0 0.8 copy_convert_fusion
  10.9 2.7 %copy-done.2 = f32[4,4,192,448]{3,2,0,1:T(8,128)} copy-done((f32[4,4,192,448]{3,2,0,1:T(8,128)}, f32[4,4,192,448]{3,2,0,1:T(8,128)S(1)}, u32[]{:S(2)}) %copy-start.2) | copy-done | bytes 5505048
  13.5 1.8 %fusion.59 = (f32[4,4,192,2]{3,2,0,1:T(8,128)S(1)}, f32[4,4,192,2]{3,2,0,1:T(8,128)}) fusion(f32[4,4,192,448]{3,2,0,1:T(8,128)S(1)} %copy_convert_fusion), kind=kLoop, calls=%fused_computation.143 | loop fusion | bytes 98304 | tf_op jit(solution)/shard_map/slice | solution.py:15
  15.3 2.0 %copy.86 = f32[4,4,192,2]{2,1,3,0:T(4,128)S(1)} copy(f32[4,4,192,2]{3,2,0,1:T(8,128)} %get-tuple-element.18) | data formatting | bytes 49152 | tf_op jit(solution)/shard_map/slice | solution.py:17
  17.3 1.4 %collective-permute-start.1 = (f32[4,4,192,2]{2,1,3,0:T(4,128)S(1)}, f32[4,4,192,2]{2,1,3,0:T(4,128)S(1)}, u32[]{:S(2)}, u32[]{:S(2)}) collective-permute-start(f32[4,4,192,2]{2,1,3,0:T(4,128)S(1)} %copy.86), channel_id=1, source_target_pairs={{1,0},{2,1},{3,2},{4,3},{5,4},{6,5},{7,6},{8,7},{9,8},{10,9},{11,1... | collective-permute-start | bytes 73736 | tf_op jit(solution)/shard_map/ppermute | solution.py:17
  18.7 0.6 copy.85
  19.6 0.7 fusion.63
  20.4 0.7 gather_fusion
  21.5 0.7 stack.27
  22.2 0.7 stack.25
  23.5 0.7 stack.26
  24.1 0.7 fusion.56
  25.2 4.4 %collective-permute-start.6 = (f32[1,2,2,452]{3,2,1,0:T(2,128)S(1)}, f32[1,2,2,452]{3,2,1,0:T(2,128)S(1)}, u32[]{:S(2)}, u32[]{:S(2)}) collective-permute-start(f32[1,2,2,452]{3,2,1,0:T(2,128)S(1)} %get-tuple-element.21), channel_id=1, source_target_pairs={{0,16},{16,32},{32,48},{48,64},{64,80},{80,96},{96,112},{1,17},{17... | collective-permute-start | bytes 21704 | tf_op jit(solution)/shard_map/ppermute | solution.py:14
  29.5 1.3 collective-permute-start.7
  30.9 4.5 %collective-permute-done.7 = f32[1,2,2,452]{3,2,1,0:T(2,128)S(1)} collective-permute-done((f32[1,2,2,452]{3,2,1,0:T(2,128)S(1)}, f32[1,2,2,452]{3,2,1,0:T(2,128)S(1)}, u32[]{:S(2)}, u32[]{:S(2)}) %collective-permute-start.7) | collective-permute-done | bytes 7264 | tf_op jit(solution)/shard_map/ppermute | solution.py:17
  35.8 1.4 %slice_bitcast_fusion.11 = (f32[194,450]{1,0:T(8,128)S(1)}, f32[194,450]{1,0:T(8,128)}, f32[194,450]{1,0:T(8,128)}, f32[194,450]{1,0:T(8,128)}) fusion(f32[2,196,452]{2,1,0:T(8,128)S(1)} %maximum_bitcast_fusion), kind=kLoop, calls=%fused_computation.100 | loop fusion | bytes 2793600 | tf_op jit(solution)/shard_map/mul | solution.py:42
  37.2 1.7 %copy.87 = f32[4,4,192,2]{3,2,0,1:T(8,128)} copy(f32[4,4,192,2]{2,1,3,0:T(4,128)S(1)} %collective-permute-done) | data formatting | bytes 49152 | tf_op jit(solution)/shard_map/ppermute | solution.py:14
  38.9 1.7 %copy.88 = f32[4,4,192,2]{3,2,0,1:T(8,128)} copy(f32[4,4,192,2]{2,1,3,0:T(4,128)S(1)} %collective-permute-done.1) | data formatting | bytes 49152 | tf_op jit(solution)/shard_map/ppermute | solution.py:17
  40.6 1.5 %pad_maximum_fusion.24 = (f32[4,4,2,452]{3,2,0,1:T(2,128)S(1)}, f32[4,4,2,452]{3,2,0,1:T(2,128)S(1)}) fusion(f32[4,4,192,2]{3,2,0,1:T(8,128)} %copy.88, f32[4,4,192,448]{3,2,0,1:T(8,128)} %copy-done.2, f32[4,4,192,2]{3,2,0,1:T(8,128)} %copy.87), kind=kLoop, calls=%fused_computation.113 | loop fusion | flops 57856 | bytes 5669888 | tf_op jit(solution)/shard_map/slice | solution.py:15
  42.1 4.6 %collective-permute-start.2 = (f32[4,4,2,452]{3,2,0,1:T(2,128)S(1)}, f32[4,4,2,452]{3,2,0,1:T(2,128)S(1)}, u32[]{:S(2)}, u32[]{:S(2)}) collective-permute-start(f32[4,4,2,452]{3,2,0,1:T(2,128)S(1)} %get-tuple-element.13), channel_id=1, source_target_pairs={{0,16},{16,32},{32,48},{48,64},{64,80},{80,96},{96,112},{1,17},{17... | collective-permute-start | bytes 173576 | tf_op jit(solution)/shard_map/ppermute | solution.py:14
  46.7 1.5 %collective-permute-start.3 = (f32[4,4,2,452]{3,2,0,1:T(2,128)S(1)}, f32[4,4,2,452]{3,2,0,1:T(2,128)S(1)}, u32[]{:S(2)}, u32[]{:S(2)}) collective-permute-start(f32[4,4,2,452]{3,2,0,1:T(2,128)S(1)} %get-tuple-element.14), channel_id=1, source_target_pairs={{16,0},{32,16},{48,32},{64,48},{80,64},{96,80},{112,96},{17,1},{33... | collective-permute-start | bytes 173576 | tf_op jit(solution)/shard_map/ppermute | solution.py:17
  48.7 5.1 %collective-permute-done.3 = f32[4,4,2,452]{3,2,0,1:T(2,128)S(1)} collective-permute-done((f32[4,4,2,452]{3,2,0,1:T(2,128)S(1)}, f32[4,4,2,452]{3,2,0,1:T(2,128)S(1)}, u32[]{:S(2)}, u32[]{:S(2)}) %collective-permute-start.3) | collective-permute-done | bytes 57888 | tf_op jit(solution)/shard_map/ppermute | solution.py:17
  53.9 3.2 %pad_maximum_fusion = f32[4,4,196,452]{3,2,0,1:T(8,128)S(1)} fusion(f32[4,4,2,452]{3,2,0,1:T(2,128)S(1)} %collective-permute-done.3, f32[4,4,192,2]{3,2,0,1:T(8,128)S(1)} %copy-done.12, f32[4,4,192,448]{3,2,0,1:T(8,128)S(1)} %bitcast.77, f32[4,4,192,2]{3,2,0,1:T(8,128)S(1)} %copy-done.10, f32[4,4,2,452]{3,2,0,1:T(2,128)S(1)} %collective-permute-done.2), kind=kLoop, calls=%fused_computation.1 | loop fusion | flops 5669888 | bytes 11339776 | tf_op jit(solution)/shard_map/concatenate | solution.py:18
  57.1 6.7 %fusion.14 = f32[4,2,194,450]{3,2,0,1:T(8,128)S(1)} fusion(f32[4,4,196,452]{3,2,0,1:T(8,128)S(1)} %pad_maximum_fusion, f32[4,4,2,452]{3,2,0,1:T(2,128)S(1)} %collective-permute-done.2, f32[4,4,192,2]{3,2,0,1:T(8,128)S(1)} %copy-done.12, f32[4,4,192,448]{3,2,0,1:T(8,128)S(1)} %bitcast.77, f32[4,4,192,2]{3,2,0,1:T(8,128)S(1)} %copy-done.10, ...), kind=kLoop, calls=%fused_computation.29 | loop fusion | flops 15364800 | bytes 21055296 | tf_op jit(solution)/shard_map/add | solution.py:48
  63.9 3.8 %fusion.60 = (f32[4,2,192,448]{3,2,0,1:T(8,128)S(1)}, f32[4,2,192,448]{3,2,0,1:T(8,128)S(1)}) fusion(f32[4,2,194,450]{3,2,0,1:T(8,128)S(1)} %fusion.14, f32[4,2,448]{2,0,1:T(4,128)S(1)} %fusion.53, f32[4,2,192]{2,0,1:T(4,128)S(1)} %get-tuple-element.42, f32[192,448]{1,0:T(8,128)S(1)} %get-tuple-element.24, f32[192,448]{1,0:T(8,128)S(1)} %get-tuple-element.25, ...), kind=kLoop, calls=%fused_computation.144 | loop fusion | flops 11010048 | bytes 23416832 | tf_op jit(solution)/shard_map/slice | solution.py:102
  67.8 2.6 %pad_maximum_fusion.17 = (f32[4,4,192,2]{3,2,0,1:T(8,128)}, f32[4,4,192,2]{3,2,0,1:T(8,128)}) fusion(f32[4,2,192,448]{3,2,0,1:T(8,128)S(1)} %get-tuple-element.20, f32[4,2,192,448]{3,2,0,1:T(8,128)S(1)} %get-tuple-element.19), kind=kLoop, calls=%fused_computation.84 | loop fusion | flops 12288 | bytes 5554176 | tf_op jit(solution)/shard_map/slice | solution.py:15
  70.4 1.0 copy-done.7
  71.4 2.2 %copy.94 = f32[4,4,192,2]{2,1,3,0:T(4,128)S(1)} copy(f32[4,4,192,2]{3,2,0,1:T(8,128)} %get-tuple-element.15) | data formatting | bytes 49152 | tf_op jit(solution)/shard_map/slice | solution.py:15
  73.6 2.0 %copy.95 = f32[4,4,192,2]{2,1,3,0:T(4,128)S(1)} copy(f32[4,4,192,2]{3,2,0,1:T(8,128)} %get-tuple-element.16) | data formatting | bytes 49152 | tf_op jit(solution)/shard_map/slice | solution.py:17
  75.7 3.6 %collective-permute-start.9 = (f32[4,4,192,2]{2,1,3,0:T(4,128)S(1)}, f32[4,4,192,2]{2,1,3,0:T(4,128)S(1)}, u32[]{:S(2)}, u32[]{:S(2)}) collective-permute-start(f32[4,4,192,2]{2,1,3,0:T(4,128)S(1)} %copy.95), channel_id=1, source_target_pairs={{1,0},{2,1},{3,2},{4,3},{5,4},{6,5},{7,6},{8,7},{9,8},{10,9},{11,1... | collective-permute-start | bytes 73736 | tf_op jit(solution)/shard_map/ppermute | solution.py:17
  79.3 0.6 dynamic_slice.9
  79.9 1.7 %copy.96 = f32[4,4,192,2]{3,2,0,1:T(8,128)} copy(f32[4,4,192,2]{2,1,3,0:T(4,128)S(1)} %collective-permute-done.8) | data formatting | bytes 49152 | tf_op jit(solution)/shard_map/ppermute | solution.py:14
  81.6 1.7 %copy.97 = f32[4,4,192,2]{3,2,0,1:T(8,128)} copy(f32[4,4,192,2]{2,1,3,0:T(4,128)S(1)} %collective-permute-done.9) | data formatting | bytes 49152 | tf_op jit(solution)/shard_map/ppermute | solution.py:17
  83.3 1.5 %pad_maximum_fusion.21 = (f32[4,4,2,452]{3,2,0,1:T(2,128)S(1)}, f32[4,4,2,452]{3,2,0,1:T(2,128)S(1)}) fusion(f32[4,4,192,2]{3,2,0,1:T(8,128)} %copy.97, f32[4,4,192,2]{3,2,0,1:T(8,128)} %copy.96, f32[4,2,192,448]{3,2,0,1:T(8,128)S(1)} %copy-done.4, f32[4,2,192,448]{3,2,0,1:T(8,128)} %copy-done.7), kind=kLoop, calls=%fused_computation.110 | loop fusion | flops 86784 | bytes 5669888 | tf_op jit(solution)/shard_map/slice | solution.py:15
  84.8 4.5 %collective-permute-start.10 = (f32[4,4,2,452]{3,2,0,1:T(2,128)S(1)}, f32[4,4,2,452]{3,2,0,1:T(2,128)S(1)}, u32[]{:S(2)}, u32[]{:S(2)}) collective-permute-start(f32[4,4,2,452]{3,2,0,1:T(2,128)S(1)} %get-tuple-element.11), channel_id=1, source_target_pairs={{0,16},{16,32},{32,48},{48,64},{64,80},{80,96},{96,112},{1,17},{17... | collective-permute-start | bytes 173576 | tf_op jit(solution)/shard_map/ppermute | solution.py:14
  89.3 1.5 %collective-permute-start.11 = (f32[4,4,2,452]{3,2,0,1:T(2,128)S(1)}, f32[4,4,2,452]{3,2,0,1:T(2,128)S(1)}, u32[]{:S(2)}, u32[]{:S(2)}) collective-permute-start(f32[4,4,2,452]{3,2,0,1:T(2,128)S(1)} %get-tuple-element.12), channel_id=1, source_target_pairs={{16,0},{32,16},{48,32},{64,48},{80,64},{96,80},{112,96},{17,1},{33... | collective-permute-start | bytes 173576 | tf_op jit(solution)/shard_map/ppermute | solution.py:17
  90.9 0.6 compare_convert_fusion
  91.6 4.3 %collective-permute-done.11 = f32[4,4,2,452]{3,2,0,1:T(2,128)S(1)} collective-permute-done((f32[4,4,2,452]{3,2,0,1:T(2,128)S(1)}, f32[4,4,2,452]{3,2,0,1:T(2,128)S(1)}, u32[]{:S(2)}, u32[]{:S(2)}) %collective-permute-start.11) | collective-permute-done | bytes 57888 | tf_op jit(solution)/shard_map/ppermute | solution.py:17
  95.9 5.3 %pad_maximum_fusion.1 = f32[4,4,196,452]{3,2,0,1:T(8,128)} fusion(f32[4,4,2,452]{3,2,0,1:T(2,128)S(1)} %collective-permute-done.11, f32[4,4,192,2]{3,2,0,1:T(8,128)S(1)} %copy-done.11, f32[4,2,192,448]{3,2,0,1:T(8,128)S(1)} %copy-done.4, f32[4,2,192,448]{3,2,0,1:T(8,128)S(1)} %copy-done.8, f32[4,4,192,2]{3,2,0,1:T(8,128)S(1)} %copy-done.9, ...), kind=kLoop, calls=%fused_computation.2 | loop fusion | flops 7087360 | bytes 11339776 | tf_op jit(solution)/shard_map/concatenate | solution.py:18
  101.2 14.1 %fusion.3 = f32[4,2,194,450]{3,2,0,1:T(8,128)S(1)} fusion(f32[4,4,196,452]{3,2,0,1:T(8,128)} %pad_maximum_fusion.1, f32[4,4,2,452]{3,2,0,1:T(2,128)S(1)} %collective-permute-done.10, f32[4,4,192,2]{3,2,0,1:T(8,128)S(1)} %copy-done.11, f32[4,4,192,2]{3,2,0,1:T(8,128)S(1)} %copy-done.9, f32[4,2,192,448]{3,2,0,1:T(8,128)S(1)} %copy-done.4, ...), kind=kLoop, calls=%fused_computation.7 | loop fusion | flops 16761600 | bytes 21055296 | tf_op jit(solution)/shard_map/add | solution.py:48
  115.4 3.8 %fusion.25 = f32[4,2,192,448]{3,2,0,1:T(8,128)S(1)} fusion(f32[4,2,194,450]{3,2,0,1:T(8,128)S(1)} %fusion.3, f32[4,2,192,448]{3,2,0,1:T(8,128)S(1)} %copy-done.4, f32[4,2,192]{2,0,1:T(4,128)S(1)} %get-tuple-element.41, f32[4,2,448]{2,0,1:T(4,128)S(1)} %copy-done.31, f32[192,448]{1,0:T(8,128)S(1)} %copy-done.24, f32[192,448]{1,0:T(8,128)S(1)} %copy-done.26, ...), kind=kLoop, calls=%fused_computation.49 | loop fusion | flops 11010048 | bytes 20664320 | tf_op jit(solution)/shard_map/add | solution.py:48
  119.2 2.4 %fusion.47 = (f32[192,448]{1,0:T(8,128)S(1)}, f32[192,448]{1,0:T(8,128)S(1)}, f32[192,448]{1,0:T(8,128)S(1)}, f32[192,448]{1,0:T(8,128)S(1)}) fusion(f32[4,2,192,448]{3,2,0,1:T(8,128)S(1)} %copy-done.4, f32[4]{0:T(128)S(1)} %compare_convert_fusion, f32[4,2,194,450]{3,2,0,1:T(8,128)S(1)} %fusion.3, f32[4,2,192,448]{3,2,0,1:T(8,128)S(1)} %fusion.25, ...), kind=kLoop, calls=%fused_computation.87 | loop fusion | flops 3784704 | bytes 12386320 | tf_op jit(solution)/shard_map/reduce_sum | solution.py:104
  121.9 9.7 %all_to_all.5 = f32[2,192,448]{2,1,0:T(8,128)S(1)} all-to-all(f32[2,192,448]{2,1,0:T(8,128)S(1)} %broadcast_in_dim.11), channel_id=1, replica_groups=mesh['pair'=2,'lat'=8,'lon'=16] {'pair'}, dimensions={0} | all-to-all | bytes 1376256 | tf_op jit(solution)/shard_map/all_to_all | solution.py:24
  131.6 0.8 reduce_sum.49
  (114 shorter events, 3.2 us)
Async XLA Ops:
  0.0 19.5 %copy-start = (f32[8,4]{0,1:T(4,128)S(1)}, f32[8,4]{0,1:T(4,128)}, u32[]{:S(2)}) copy-start(f32[8,4]{0,1:T(4,128)} %param.11) | copy-start | bytes 388
  0.0 10.0 %copy-start.29 = (bf16[4,4,192,448]{3,2,1,0:T(8,128)(2,1)S(1)}, bf16[4,4,192,448]{3,2,1,0:T(8,128)(2,1)}, u32[]{:S(2)}) copy-start(bf16[4,4,192,448]{3,2,1,0:T(8,128)(2,1)} %param.8) | copy-start | bytes 8257540
  2.5 22.6 %collective-permute-start.4 = (f32[1,2,192,2]{3,2,1,0:T(8,128)S(1)}, f32[1,2,192,2]{3,2,1,0:T(8,128)S(1)}, u32[]{:S(2)}, u32[]{:S(2)}) collective-permute-start(f32[1,2,192,2]{3,2,1,0:T(8,128)S(1)} %get-tuple-element.31), channel_id=1, source_target_pairs={{0,1},{1,2},{2,3},{3,4},{4,5},{5,6},{6,7},{7,8},{8,9},{9,10},{10,1... | collective-permute-start | bytes 9224 | tf_op jit(solution)/shard_map/ppermute | solution.py:14
  4.6 20.4 %collective-permute-start.5 = (f32[1,2,192,2]{3,2,1,0:T(8,128)S(1)}, f32[1,2,192,2]{3,2,1,0:T(8,128)S(1)}, u32[]{:S(2)}, u32[]{:S(2)}) collective-permute-start(f32[1,2,192,2]{3,2,1,0:T(8,128)S(1)} %get-tuple-element.32), channel_id=1, source_target_pairs={{1,0},{2,1},{3,2},{4,3},{5,4},{6,5},{7,6},{8,7},{9,8},{10,9},{11,1... | collective-permute-start | bytes 9224 | tf_op jit(solution)/shard_map/ppermute | solution.py:17
  13.5 6.0 %copy-start.36 = (s32[8,2]{0,1:T(2,128)S(1)}, s32[8,2]{0,1:T(2,128)}, u32[]{:S(2)}) copy-start(s32[8,2]{0,1:T(2,128)} %param.9) | copy-start | bytes 196
  13.5 6.1 %copy-start.35 = (f32[4]{0:T(128)S(1)}, f32[4]{0:T(128)}, u32[]{:S(2)}) copy-start(f32[4]{0:T(128)} %param.13) | copy-start | bytes 52
  13.5 6.9 %copy-start.1 = (s32[256]{0:T(256)S(1)}, s32[256]{0:T(256)}, u32[]{:S(2)}) copy-start(s32[256]{0:T(256)} %param.12) | copy-start | bytes 3076
  17.3 21.6 %collective-permute-start.1 = (f32[4,4,192,2]{2,1,3,0:T(4,128)S(1)}, f32[4,4,192,2]{2,1,3,0:T(4,128)S(1)}, u32[]{:S(2)}, u32[]{:S(2)}) collective-permute-start(f32[4,4,192,2]{2,1,3,0:T(4,128)S(1)} %copy.86), channel_id=1, source_target_pairs={{1,0},{2,1},{3,2},{4,3},{5,4},{6,5},{7,6},{8,7},{9,8},{10,9},{11,1... | collective-permute-start | bytes 73736 | tf_op jit(solution)/shard_map/ppermute | solution.py:17
  19.4 17.8 %collective-permute-start = (f32[4,4,192,2]{2,1,3,0:T(4,128)S(1)}, f32[4,4,192,2]{2,1,3,0:T(4,128)S(1)}, u32[]{:S(2)}, u32[]{:S(2)}) collective-permute-start(f32[4,4,192,2]{2,1,3,0:T(4,128)S(1)} %copy.85), channel_id=1, source_target_pairs={{0,1},{1,2},{2,3},{3,4},{4,5},{5,6},{6,7},{7,8},{8,9},{9,10},{10,1... | collective-permute-start | bytes 73736 | tf_op jit(solution)/shard_map/ppermute | solution.py:14
  25.0 32.1 %copy-start.32 = (f32[4,2,450]{2,0,1:T(4,128)}, f32[4,2,450]{2,0,1:T(4,128)S(1)}, u32[]{:S(2)}) copy-start(f32[4,2,450]{2,0,1:T(4,128)S(1)} %fusion.52) | copy-start | bytes 43204
  25.2 5.7 %collective-permute-start.6 = (f32[1,2,2,452]{3,2,1,0:T(2,128)S(1)}, f32[1,2,2,452]{3,2,1,0:T(2,128)S(1)}, u32[]{:S(2)}, u32[]{:S(2)}) collective-permute-start(f32[1,2,2,452]{3,2,1,0:T(2,128)S(1)} %get-tuple-element.21), channel_id=1, source_target_pairs={{0,16},{16,32},{32,48},{48,64},{64,80},{80,96},{96,112},{1,17},{17... | collective-permute-start | bytes 21704 | tf_op jit(solution)/shard_map/ppermute | solution.py:14
  29.5 5.9 %collective-permute-start.7 = (f32[1,2,2,452]{3,2,1,0:T(2,128)S(1)}, f32[1,2,2,452]{3,2,1,0:T(2,128)S(1)}, u32[]{:S(2)}, u32[]{:S(2)}) collective-permute-start(f32[1,2,2,452]{3,2,1,0:T(2,128)S(1)} %get-tuple-element.22), channel_id=1, source_target_pairs={{16,0},{32,16},{48,32},{64,48},{80,64},{96,80},{112,96},{17,1},{33... | collective-permute-start | bytes 21704 | tf_op jit(solution)/shard_map/ppermute | solution.py:17
  30.9 33.0 %copy-start.30 = (f32[4,2,448]{2,0,1:T(4,128)}, f32[4,2,448]{2,0,1:T(4,128)S(1)}, u32[]{:S(2)}) copy-start(f32[4,2,448]{2,0,1:T(4,128)S(1)} %fusion.53) | copy-start | bytes 43012
  37.2 19.9 %copy-start.13 = (f32[194,450]{1,0:T(8,128)}, f32[194,450]{1,0:T(8,128)S(1)}, u32[]{:S(2)}) copy-start(f32[194,450]{1,0:T(8,128)S(1)} %get-tuple-element.27) | copy-start | bytes 1047604
  38.9 15.0 %slice-start = ((s8[6291456]{0:T(1024)(128)(4,1)}), s8[2097152]{0:T(1024)(128)(4,1)S(1)}, s32[]{:S(2)}) async-start(s8[6291456]{0:T(1024)(128)(4,1)} %bitcast.76), calls=%async_computation.1 | async-start | bytes 4194304
  40.6 13.3 %slice-start.1 = ((s8[6291456]{0:T(1024)(128)(4,1)}), s8[4194304]{0:T(1024)(128)(4,1)S(1)}, s32[]{:S(2)}) async-start(s8[6291456]{0:T(1024)(128)(4,1)} %bitcast.76), calls=%async_computation.2 | async-start | bytes 8388608
  42.1 11.8 %copy-start.10 = (f32[4,4,192,2]{3,2,0,1:T(8,128)S(1)}, f32[4,4,192,2]{3,2,0,1:T(8,128)}, u32[]{:S(2)}) copy-start(f32[4,4,192,2]{3,2,0,1:T(8,128)} %copy.87) | copy-start | bytes 73732
  42.1 11.8 %copy-start.12 = (f32[4,4,192,2]{3,2,0,1:T(8,128)S(1)}, f32[4,4,192,2]{3,2,0,1:T(8,128)}, u32[]{:S(2)}) copy-start(f32[4,4,192,2]{3,2,0,1:T(8,128)} %copy.88) | copy-start | bytes 73732
  42.1 6.7 %collective-permute-start.2 = (f32[4,4,2,452]{3,2,0,1:T(2,128)S(1)}, f32[4,4,2,452]{3,2,0,1:T(2,128)S(1)}, u32[]{:S(2)}, u32[]{:S(2)}) collective-permute-start(f32[4,4,2,452]{3,2,0,1:T(2,128)S(1)} %get-tuple-element.13), channel_id=1, source_target_pairs={{0,16},{16,32},{32,48},{48,64},{64,80},{80,96},{96,112},{1,17},{17... | collective-permute-start | bytes 173576 | tf_op jit(solution)/shard_map/ppermute | solution.py:14
  46.7 7.1 %collective-permute-start.3 = (f32[4,4,2,452]{3,2,0,1:T(2,128)S(1)}, f32[4,4,2,452]{3,2,0,1:T(2,128)S(1)}, u32[]{:S(2)}, u32[]{:S(2)}) collective-permute-start(f32[4,4,2,452]{3,2,0,1:T(2,128)S(1)} %get-tuple-element.14), channel_id=1, source_target_pairs={{16,0},{32,16},{48,32},{64,48},{80,64},{96,80},{112,96},{17,1},{33... | collective-permute-start | bytes 173576 | tf_op jit(solution)/shard_map/ppermute | solution.py:17
  48.7 15.2 %copy-start.21 = (f32[192,448]{1,0:T(8,128)}, f32[192,448]{1,0:T(8,128)S(1)}, u32[]{:S(2)}) copy-start(f32[192,448]{1,0:T(8,128)S(1)} %get-tuple-element.23) | copy-start | bytes 1032196
  48.7 15.2 %copy-start.23 = (f32[192,448]{1,0:T(8,128)}, f32[192,448]{1,0:T(8,128)S(1)}, u32[]{:S(2)}) copy-start(f32[192,448]{1,0:T(8,128)S(1)} %get-tuple-element.24) | copy-start | bytes 1032196
  48.7 15.2 %copy-start.25 = (f32[192,448]{1,0:T(8,128)}, f32[192,448]{1,0:T(8,128)S(1)}, u32[]{:S(2)}) copy-start(f32[192,448]{1,0:T(8,128)S(1)} %get-tuple-element.25) | copy-start | bytes 1032196
  48.7 15.2 %copy-start.27 = (f32[192,448]{1,0:T(8,128)}, f32[192,448]{1,0:T(8,128)S(1)}, u32[]{:S(2)}) copy-start(f32[192,448]{1,0:T(8,128)S(1)} %get-tuple-element.26) | copy-start | bytes 1032196
  48.7 8.4 %copy-start.15 = (f32[194,450]{1,0:T(8,128)S(1)}, f32[194,450]{1,0:T(8,128)}, u32[]{:S(2)}) copy-start(f32[194,450]{1,0:T(8,128)} %get-tuple-element.28) | copy-start | bytes 1047604
  48.7 8.4 %copy-start.17 = (f32[194,450]{1,0:T(8,128)S(1)}, f32[194,450]{1,0:T(8,128)}, u32[]{:S(2)}) copy-start(f32[194,450]{1,0:T(8,128)} %get-tuple-element.29) | copy-start | bytes 1047604
  48.7 8.4 %copy-start.19 = (f32[194,450]{1,0:T(8,128)S(1)}, f32[194,450]{1,0:T(8,128)}, u32[]{:S(2)}) copy-start(f32[194,450]{1,0:T(8,128)} %get-tuple-element.30) | copy-start | bytes 1047604
  63.9 3.9 %copy-start.5 = (f32[4,2,194,450]{3,2,0,1:T(8,128)}, f32[4,2,194,450]{3,2,0,1:T(8,128)S(1)}, u32[]{:S(2)}) copy-start(f32[4,2,194,450]{3,2,0,1:T(8,128)S(1)} %fusion.14) | copy-start | bytes 8380804
  67.8 11.5 %copy-start.37 = (s32[2]{0:T(128)S(1)}, s32[2]{0:T(128)}, u32[]{:S(2)}) copy-start(s32[2]{0:T(128)} %param.10) | copy-start | bytes 28
  71.4 11.9 %copy-start.4 = (f32[4,2,192,448]{3,2,0,1:T(8,128)S(1)}, f32[4,2,192,448]{3,2,0,1:T(8,128)}, u32[]{:S(2)}) copy-start(f32[4,2,192,448]{3,2,0,1:T(8,128)} %copy-done.3) | copy-start | bytes 8257540
  73.6 6.3 %collective-permute-start.8 = (f32[4,4,192,2]{2,1,3,0:T(4,128)S(1)}, f32[4,4,192,2]{2,1,3,0:T(4,128)S(1)}, u32[]{:S(2)}, u32[]{:S(2)}) collective-permute-start(f32[4,4,192,2]{2,1,3,0:T(4,128)S(1)} %copy.94), channel_id=1, source_target_pairs={{0,1},{1,2},{2,3},{3,4},{4,5},{5,6},{6,7},{7,8},{8,9},{9,10},{10,1... | collective-permute-start | bytes 73736 | tf_op jit(solution)/shard_map/ppermute | solution.py:14
  75.7 6.0 %collective-permute-start.9 = (f32[4,4,192,2]{2,1,3,0:T(4,128)S(1)}, f32[4,4,192,2]{2,1,3,0:T(4,128)S(1)}, u32[]{:S(2)}, u32[]{:S(2)}) collective-permute-start(f32[4,4,192,2]{2,1,3,0:T(4,128)S(1)} %copy.95), channel_id=1, source_target_pairs={{1,0},{2,1},{3,2},{4,3},{5,4},{6,5},{7,6},{8,7},{9,8},{10,9},{11,1... | collective-permute-start | bytes 73736 | tf_op jit(solution)/shard_map/ppermute | solution.py:17
  83.3 12.5 %copy-start.8 = (f32[4,2,192,448]{3,2,0,1:T(8,128)S(1)}, f32[4,2,192,448]{3,2,0,1:T(8,128)}, u32[]{:S(2)}) copy-start(f32[4,2,192,448]{3,2,0,1:T(8,128)} %copy-done.7) | copy-start | bytes 8257540
  83.3 12.5 %copy-start.9 = (f32[4,4,192,2]{3,2,0,1:T(8,128)S(1)}, f32[4,4,192,2]{3,2,0,1:T(8,128)}, u32[]{:S(2)}) copy-start(f32[4,4,192,2]{3,2,0,1:T(8,128)} %copy.96) | copy-start | bytes 73732
  83.3 12.5 %copy-start.11 = (f32[4,4,192,2]{3,2,0,1:T(8,128)S(1)}, f32[4,4,192,2]{3,2,0,1:T(8,128)}, u32[]{:S(2)}) copy-start(f32[4,4,192,2]{3,2,0,1:T(8,128)} %copy.97) | copy-start | bytes 73732
  84.8 6.7 %collective-permute-start.10 = (f32[4,4,2,452]{3,2,0,1:T(2,128)S(1)}, f32[4,4,2,452]{3,2,0,1:T(2,128)S(1)}, u32[]{:S(2)}, u32[]{:S(2)}) collective-permute-start(f32[4,4,2,452]{3,2,0,1:T(2,128)S(1)} %get-tuple-element.11), channel_id=1, source_target_pairs={{0,16},{16,32},{32,48},{48,64},{64,80},{80,96},{96,112},{1,17},{17... | collective-permute-start | bytes 173576 | tf_op jit(solution)/shard_map/ppermute | solution.py:14
  89.3 6.5 %collective-permute-start.11 = (f32[4,4,2,452]{3,2,0,1:T(2,128)S(1)}, f32[4,4,2,452]{3,2,0,1:T(2,128)S(1)}, u32[]{:S(2)}, u32[]{:S(2)}) collective-permute-start(f32[4,4,2,452]{3,2,0,1:T(2,128)S(1)} %get-tuple-element.12), channel_id=1, source_target_pairs={{16,0},{32,16},{48,32},{64,48},{80,64},{96,80},{112,96},{17,1},{33... | collective-permute-start | bytes 173576 | tf_op jit(solution)/shard_map/ppermute | solution.py:17
  91.5 9.6 %copy-start.14 = (f32[194,450]{1,0:T(8,128)S(1)}, f32[194,450]{1,0:T(8,128)}, u32[]{:S(2)}) copy-start(f32[194,450]{1,0:T(8,128)} %copy-done.13) | copy-start | bytes 1047604
  91.5 9.6 %copy-start.16 = (f32[194,450]{1,0:T(8,128)S(1)}, f32[194,450]{1,0:T(8,128)}, u32[]{:S(2)}) copy-start(f32[194,450]{1,0:T(8,128)} %get-tuple-element.28) | copy-start | bytes 1047604
  91.5 9.6 %copy-start.18 = (f32[194,450]{1,0:T(8,128)S(1)}, f32[194,450]{1,0:T(8,128)}, u32[]{:S(2)}) copy-start(f32[194,450]{1,0:T(8,128)} %get-tuple-element.29) | copy-start | bytes 1047604
  91.5 9.6 %copy-start.20 = (f32[194,450]{1,0:T(8,128)S(1)}, f32[194,450]{1,0:T(8,128)}, u32[]{:S(2)}) copy-start(f32[194,450]{1,0:T(8,128)} %get-tuple-element.30) | copy-start | bytes 1047604
  91.5 9.6 %copy-start.33 = (f32[4,2,450]{2,0,1:T(4,128)S(1)}, f32[4,2,450]{2,0,1:T(4,128)}, u32[]{:S(2)}) copy-start(f32[4,2,450]{2,0,1:T(4,128)} %copy-done.32) | copy-start | bytes 43204
  91.6 9.6 %copy-start.34 = (f32[4,2,194]{2,0,1:T(4,128)S(1)}, f32[4,2,194]{2,0,1:T(4,128)}, u32[]{:S(2)}) copy-start(f32[4,2,194]{2,0,1:T(4,128)} %get-tuple-element.43) | copy-start | bytes 18628
  101.2 14.2 %copy-start.22 = (f32[192,448]{1,0:T(8,128)S(1)}, f32[192,448]{1,0:T(8,128)}, u32[]{:S(2)}) copy-start(f32[192,448]{1,0:T(8,128)} %copy-done.21) | copy-start | bytes 1032196
  101.2 14.2 %copy-start.24 = (f32[192,448]{1,0:T(8,128)S(1)}, f32[192,448]{1,0:T(8,128)}, u32[]{:S(2)}) copy-start(f32[192,448]{1,0:T(8,128)} %copy-done.23) | copy-start | bytes 1032196
  101.2 14.2 %copy-start.26 = (f32[192,448]{1,0:T(8,128)S(1)}, f32[192,448]{1,0:T(8,128)}, u32[]{:S(2)}) copy-start(f32[192,448]{1,0:T(8,128)} %copy-done.25) | copy-start | bytes 1032196
  101.2 14.2 %copy-start.28 = (f32[192,448]{1,0:T(8,128)S(1)}, f32[192,448]{1,0:T(8,128)}, u32[]{:S(2)}) copy-start(f32[192,448]{1,0:T(8,128)} %copy-done.27) | copy-start | bytes 1032196
  101.2 14.2 %copy-start.31 = (f32[4,2,448]{2,0,1:T(4,128)S(1)}, f32[4,2,448]{2,0,1:T(4,128)}, u32[]{:S(2)}) copy-start(f32[4,2,448]{2,0,1:T(4,128)} %copy-done.30) | copy-start | bytes 43012
  (4 other events, 12.7 us)
where the time goes:
time: 133 us; the launch traced here: 132 us
  other arithmetic  51.1 us (38%)
  starting transfers between devices  30.5 us (23%)
  local copies, waits for them, and re-layouts  26.6 us (20%)
  waiting for transfers between devices  13.9 us (10%)
  blocking collectives  9.71 us (7%)
    add x3, other arithmetic, advance(): return 2.0 * centre - earlier + change + source  24.6 us
    ppermute x6, starting transfers between devices, extended(): lax.ppermute(lax.slice_in_dim(block, block.shape[dim] - width, None, axis...  15.8 us
    ppermute x6, starting transfers between devices, extended(): lax.ppermute(lax.slice_in_dim(block, 0, width, axis=dim), axis, backward)  14.7 us
    ppermute x6, waiting for transfers between devices, extended(): lax.ppermute(lax.slice_in_dim(block, 0, width, axis=dim), axis, backward)  13.9 us
    all_to_all x1, blocking collectives, copy_for_each(): lax.all_to_all(jnp.broadcast_to(x[None], (devices, *x.shape)), axis, 0, 0...  9.71 us
    concatenate x2, other arithmetic, extended(): block = jnp.concatenate([low, block, high], axis=dim)  8.46 us
    slice x4, other arithmetic, extended(): lax.slice_in_dim(block, block.shape[dim] - width, None, axis=dim)  5.65 us
    slice x4, local copies, waits for them, and re-layouts, extended(): lax.slice_in_dim(block, block.shape[dim] - width, None, axis=dim)  4.66 us
  transfers between devices with their start and end apart: 12, of which 3 were waited for; matrix products, arithmetic and copies ran while one was open for 15% of the time, Pallas kernels for 0%

commit v1 on v0

v1 whole, which is shorter than its diff:
```python
import functools

import jax
import jax.numpy as jnp
from jax import lax
from jax.experimental import pallas as pl
from jax.experimental.pallas import tpu as pltpu
from jax.sharding import PartitionSpec as P

HALO = 4
TOP = 16
COLS = 512
STRIP = 8
MESH = pl.DeviceIdType.MESH


def exchange_kernel(send_l, send_r, top_rows, bot_rows, out_l, out_r, out_a, out_b, rl, rr, ra, rb, st, sb, send_sem, recv_sem):
    nlon = lax.axis_size("lon")
    nlat = lax.axis_size("lat")
    me_lat = lax.axis_index("lat")
    me_lon = lax.axis_index("lon")
    right = lax.rem(me_lon + 1, nlon)
    left = lax.rem(me_lon + nlon - 1, nlon)
    has_up = me_lat > 0
    has_down = me_lat < nlat - 1
    up = jnp.maximum(me_lat - 1, 0)
    down = jnp.minimum(me_lat + 1, nlat - 1)

    barrier = pltpu.get_barrier_semaphore()
    pl.semaphore_signal(barrier, 1, device_id={"lon": left}, device_id_type=MESH)
    pl.semaphore_signal(barrier, 1, device_id={"lon": right}, device_id_type=MESH)

    @pl.when(has_up)
    def _():
        pl.semaphore_signal(barrier, 1, device_id={"lat": up}, device_id_type=MESH)

    @pl.when(has_down)
    def _():
        pl.semaphore_signal(barrier, 1, device_id={"lat": down}, device_id_type=MESH)

    pl.semaphore_wait(barrier, 2 + has_up.astype(jnp.int32) + has_down.astype(jnp.int32))

    to_right = pltpu.make_async_remote_copy(send_r, rl, send_sem.at[0], recv_sem.at[0], device_id={"lon": right}, device_id_type=MESH)
    to_left = pltpu.make_async_remote_copy(send_l, rr, send_sem.at[1], recv_sem.at[1], device_id={"lon": left}, device_id_type=MESH)
    to_right.start()
    to_left.start()
    to_right.wait()
    to_left.wait()

    lane = lax.broadcasted_iota(jnp.int32, (STRIP, 128), 1)
    east_gap = (lane >= 64) & (lane < 64 + HALO)
    west_gap = lane >= 128 - HALO
    rows = rl.shape[0]
    for dst, src, first in ((st, top_rows, 0), (sb, bot_rows, rows - STRIP)):
        dst[...] = src[...]
        from_r = rr[pl.ds(first, STRIP), :]
        from_l = rl[pl.ds(first, STRIP), :]
        for a in range(src.shape[0]):
            hr = pltpu.roll(from_r, (64 - HALO * a) % 128, 1)
            hl = pltpu.roll(from_l, (128 - HALO - HALO * a) % 128, 1)
            tail = dst[a, :, pl.ds(384, 128)]
            dst[a, :, pl.ds(384, 128)] = jnp.where(east_gap, hr, jnp.where(west_gap, hl, tail))

    def upward():
        return pltpu.make_async_remote_copy(st, rb, send_sem.at[2], recv_sem.at[2], device_id={"lat": up}, device_id_type=MESH)

    def downward():
        return pltpu.make_async_remote_copy(sb, ra, send_sem.at[3], recv_sem.at[3], device_id={"lat": down}, device_id_type=MESH)

    @pl.when(has_up)
    def _():
        upward().start()

    @pl.when(has_down)
    def _():
        downward().start()

    @pl.when(has_up)
    def _():
        upward().wait_send()
        downward().wait_recv()

    @pl.when(has_down)
    def _():
        downward().wait_send()
        upward().wait_recv()

    @pl.when(jnp.logical_not(has_up))
    def _():
        ra[...] = jnp.zeros_like(ra)

    @pl.when(jnp.logical_not(has_down))
    def _():
        rb[...] = jnp.zeros_like(rb)

    out_l[...] = rl[...]
    out_r[...] = rr[...]
    out_a[...] = ra[...]
    out_b[...] = rb[...]


def exchange(send_l, send_r, top_rows, bot_rows):
    vmem = pl.BlockSpec(memory_space=pltpu.VMEM)
    shapes = [jax.ShapeDtypeStruct(x.shape, x.dtype) for x in (send_l, send_r, top_rows, bot_rows)]
    return pl.pallas_call(
        exchange_kernel,
        out_shape=shapes,
        in_specs=[vmem] * 4,
        out_specs=[vmem] * 4,
        scratch_shapes=[
            pltpu.VMEM(send_l.shape, jnp.float32),
            pltpu.VMEM(send_l.shape, jnp.float32),
            pltpu.VMEM(top_rows.shape, jnp.float32),
            pltpu.VMEM(top_rows.shape, jnp.float32),
            pltpu.VMEM(top_rows.shape, jnp.float32),
            pltpu.VMEM(top_rows.shape, jnp.float32),
            pltpu.SemaphoreType.DMA((4,)),
            pltpu.SemaphoreType.DMA((4,)),
        ],
        compiler_params=pltpu.CompilerParams(collective_id=0, has_side_effects=True),
    )(send_l, send_r, top_rows, bot_rows)


def wave_kernel(
    height,
    breadth,
    nlon,
    pl_ref,
    pc_ref,
    res_ref,
    sc_ref,
    wav_ref,
    f_ref,
    north_ref,
    east_ref,
    from_l,
    from_r,
    from_a,
    from_b,
    o_ref,
    cn,
    ca,
    ce,
    cw,
    cd,
    acc,
    bufs,
    halo,
):
    s = pl.program_id(0)
    rows = cn.shape[0]
    steps = wav_ref.shape[0]
    slots = pl.num_programs(0)
    fields = f_ref.shape[1]
    lane = lax.broadcasted_iota(jnp.int32, (height, 128), 1)

    def assemble(dst, raw, a):
        dst[pl.ds(TOP, height), pl.ds(0, breadth)] = raw
        tail = dst[pl.ds(TOP, height), pl.ds(384, 128)]
        dst[pl.ds(TOP, height), pl.ds(384, 128)] = jnp.where(lane < breadth - 384, tail, halo[a])
        dst[pl.ds(TOP - STRIP, STRIP), :] = from_a[a]
        dst[pl.ds(TOP + height, STRIP), :] = from_b[a]
        dst[pl.ds(0, TOP - STRIP), :] = jnp.zeros((TOP - STRIP, COLS), jnp.float32)
        dst[pl.ds(TOP + height + STRIP, rows - TOP - height - STRIP), :] = jnp.zeros(
            (rows - TOP - height - STRIP, COLS), jnp.float32
        )

    @pl.when(s == 0)
    def _():
        fr = from_r[...]
        fl = from_l[...]
        east_gap = (lane >= breadth - 384) & (lane < breadth - 384 + HALO)
        west_gap = lane >= 128 - HALO
        for a in range(halo.shape[0]):
            hr = pltpu.roll(fr, (breadth - 384 - HALO * a) % 128, 1)
            hl = pltpu.roll(fl, (128 - HALO - HALO * a) % 128, 1)
            halo[a] = jnp.where(east_gap, hr, jnp.where(west_gap, hl, jnp.float32(0.0)))
        coef_base = slots * fields
        assemble(cn, north_ref[...], coef_base)
        assemble(ce, east_ref[...], coef_base + 1)

        @pl.when(lax.axis_index("lat") == lax.axis_size("lat") - 1)
        def _():
            last = TOP + height - 8
            sub8 = lax.broadcasted_iota(jnp.int32, (8, COLS), 0)
            cn[pl.ds(last, 8), :] = jnp.where(sub8 == 7, jnp.float32(0.0), cn[pl.ds(last, 8), :])

        zero8 = jnp.zeros((8, COLS), jnp.float32)
        ca[pl.ds(8, rows - 16), :] = cn[pl.ds(7, rows - 16), :]
        ca[pl.ds(0, 8), :] = zero8
        ca[pl.ds(rows - 8, 8), :] = zero8
        cw[...] = pltpu.roll(ce[...], 1, 1)
        cd[...] = 2.0 - (cn[...] + ca[...] + ce[...] + cw[...])
        acc[...] = jnp.zeros_like(acc)

    member = lax.axis_index("pair")
    row_first = lax.axis_index("lat") * height
    col_first = lax.axis_index("lon") * breadth
    slot = member * slots + s
    act = jnp.where(s < pc_ref[member], jnp.float32(1.0), jnp.float32(0.0))

    places = []
    for comp in range(2):
        cell = sc_ref[pl_ref[slot * 2 + comp]]
        r = lax.div(cell, nlon)
        c = cell - r * nlon
        rb = r - row_first + TOP
        d = c - col_first
        d = jnp.where(d < 0, d + nlon, d)
        near = d < breadth + HALO
        wrap = d >= nlon - HALO
        cb = jnp.where(near, d, d - nlon + COLS)
        valid = (rb >= TOP - HALO) & (rb < TOP + height + HALO) & (near | wrap)
        places.append((rb, cb, valid))

    for comp in range(2):
        assemble(bufs.at[comp, 0], f_ref[0, comp].astype(jnp.float32), s * fields + comp)
        assemble(bufs.at[comp, 1], f_ref[0, 2 + comp].astype(jnp.float32), s * fields + 2 + comp)

    sub = lax.broadcasted_iota(jnp.int32, (8, COLS), 0)
    lane8 = lax.broadcasted_iota(jnp.int32, (8, COLS), 1)
    blocks = rows // 8

    for t in range(steps):
        ei, ci, ni = t % 3, (t + 1) % 3, (t + 2) % 3
        for comp in range(2):
            rb, cb, valid = places[comp]
            amp = wav_ref[t] if comp == 0 else res_ref[slot * steps + steps - 1 - t]

            @pl.when(valid)
            def _():
                r8 = pl.multiple_of(lax.div(rb, 8) * 8, 8)
                slab = bufs[comp, ei, pl.ds(r8, 8), :]
                hit = (sub == rb - r8) & (lane8 == cb)
                bufs[comp, ei, pl.ds(r8, 8), :] = slab - jnp.where(hit, amp, jnp.float32(0.0))

        last = t == steps - 1
        first_block, end_block = (2, blocks - 2) if last else (1, blocks - 1)
        for k in range(first_block, end_block):
            r0 = 8 * k
            dd = cd[pl.ds(r0, 8), :]
            nn = cn[pl.ds(r0, 8), :]
            aa = ca[pl.ds(r0, 8), :]
            ee = ce[pl.ds(r0, 8), :]
            ww = cw[pl.ds(r0, 8), :]
            outs = []
            for comp in range(2):
                cur = bufs[comp, ci, pl.ds(r0, 8), :]
                above = bufs[comp, ci, pl.ds(r0 - 1, 8), :]
                below = bufs[comp, ci, pl.ds(r0 + 1, 8), :]
                ear = bufs[comp, ei, pl.ds(r0, 8), :]
                west = pltpu.roll(cur, 1, 1)
                east = pltpu.roll(cur, COLS - 1, 1)
                nxt = dd * cur + nn * below + aa * above + ee * east + ww * west - ear
                bufs[comp, ni, pl.ds(r0, 8), :] = nxt
                outs.append(nxt)
            if 2 <= k < blocks - 2:
                acc[pl.ds(r0 - TOP, 8), :] += (outs[0] * act) * outs[1]

    @pl.when(s == slots - 1)
    def _():
        o_ref[...] = acc[:, pl.ds(0, breadth)]


def propagate(wave_states, lat_faces, lon_faces, halos, scalars, nlon):
    slots, fields, height, breadth = wave_states.shape
    rows = height + 2 * TOP
    smem = pl.BlockSpec(memory_space=pltpu.SMEM)
    whole2 = lambda x: pl.BlockSpec(x.shape, lambda s: (0,) * x.ndim)
    from_l, from_r, from_a, from_b = halos
    return pl.pallas_call(
        functools.partial(wave_kernel, height, breadth, nlon),
        out_shape=jax.ShapeDtypeStruct((height, breadth), jnp.float32),
        grid=(slots,),
        in_specs=[smem] * 5
        + [
            pl.BlockSpec((1, fields, height, breadth), lambda s: (s, 0, 0, 0)),
            whole2(lat_faces),
            whole2(lon_faces),
            whole2(from_l),
            whole2(from_r),
            whole2(from_a),
            whole2(from_b),
        ],
        out_specs=pl.BlockSpec((height, breadth), lambda s: (0, 0)),
        scratch_shapes=[
            pltpu.VMEM((rows, COLS), jnp.float32),
            pltpu.VMEM((rows, COLS), jnp.float32),
            pltpu.VMEM((rows, COLS), jnp.float32),
            pltpu.VMEM((rows, COLS), jnp.float32),
            pltpu.VMEM((rows, COLS), jnp.float32),
            pltpu.VMEM((height, COLS), jnp.float32),
            pltpu.VMEM((2, 3, rows, COLS), jnp.float32),
            pltpu.VMEM((from_a.shape[0], height, 128), jnp.float32),
        ],
        compiler_params=pltpu.CompilerParams(dimension_semantics=("arbitrary",)),
    )(*scalars, wave_states, lat_faces, lon_faces, from_l, from_r, from_a, from_b)


def edge_columns(fields, lat_faces, lon_faces, cols):
    x = jnp.concatenate(
        [fields[:, :, cols].astype(jnp.float32), jnp.stack([lat_faces[:, cols], lon_faces[:, cols]])]
    )
    x = jnp.transpose(x, (1, 0, 2)).reshape(x.shape[1], -1)
    return jnp.pad(x, ((0, 0), (0, 128 - x.shape[1])))


def edge_rows(fields, lat_faces, lon_faces, rows):
    x = jnp.concatenate(
        [fields[:, rows, :].astype(jnp.float32), jnp.stack([lat_faces[rows], lon_faces[rows]])]
    )
    return jnp.pad(x, ((0, 0), (0, 0), (0, COLS - x.shape[2])))


def body(
    wave_states,
    pair_list,
    pair_counts,
    residuals,
    station_cell,
    source_wavelet,
    lat_faces,
    lon_faces,
):
    height, breadth = lat_faces.shape
    nlon = breadth * lax.axis_size("lon")
    slots, fields = wave_states.shape[:2]
    flat = wave_states.reshape(slots * fields, height, breadth)
    send_l = edge_columns(flat, lat_faces, lon_faces, slice(0, HALO))
    send_r = edge_columns(flat, lat_faces, lon_faces, slice(breadth - HALO, breadth))
    top_rows = edge_rows(flat, lat_faces, lon_faces, slice(0, STRIP))
    bot_rows = edge_rows(flat, lat_faces, lon_faces, slice(height - STRIP, height))
    halos = exchange(send_l, send_r, top_rows, bot_rows)
    scalars = (pair_list.reshape(-1), pair_counts, residuals.reshape(-1), station_cell, source_wavelet)
    partial = propagate(wave_states, lat_faces, lon_faces, halos, scalars, nlon)
    other = lax.ppermute(partial, "pair", [(0, 1), (1, 0)])
    return partial + other


def solution(mesh):
    in_specs = (
        P("pair", None, "lat", "lon"),
        P(),
        P(),
        P(),
        P(),
        P(),
        P("lat", "lon"),
        P("lat", "lon"),
    )
    out_specs = P("lat", "lon")
    return jax.shard_map(body, mesh=mesh, in_specs=in_specs, out_specs=out_specs, check_vma=False)
```

time: 133 us -> 70.5 us (0.53)
  the two profiles are of different devices: /device:TPU:1 before, /device:TPU:9 now
where the time goes in v1:
time: 70.5 us; the launch traced here: 69.9 us
  Pallas kernels  40.3 us (57%)
  local copies, waits for them, and re-layouts  18.3 us (26%)
  other arithmetic  7.13 us (10%)
  starting transfers between devices  2.55 us (4%)
  waiting for transfers between devices  1.56 us (2%)
    pallas_call x1, Pallas kernels, exchange(): pl.pallas_call(exchange_kernel, out_shape=shapes, in_specs=[vmem] * 4, ou...  27 us
    pallas_call x1, Pallas kernels, propagate(): pl.pallas_call(functools.partial(wave_kernel, height, breadth, nlon), out...  13.3 us
    unnamed x10, local copies, waits for them, and re-layouts  6.88 us
    ppermute x1, starting transfers between devices, body(): other = lax.ppermute(partial, 'pair', [(0, 1), (1, 0)])  2.55 us
    another operation x2, local copies, waits for them, and re-layouts, edge_rows(): jnp.stack([lat_faces[rows], lon_faces[rows]])  2.07 us
    convert_element_type x2, local copies, waits for them, and re-layouts, edge_columns(): fields[:, :, cols].astype(jnp.float32)  1.87 us
    add x1, other arithmetic, body(): return partial + other  1.8 us
    convert_element_type x1, other arithmetic, edge_columns(): fields[:, :, cols].astype(jnp.float32)  1.79 us
  transfers between devices with their start and end apart: 1, of which 1 were waited for; matrix products, arithmetic and copies ran while one was open for 0% of the time, Pallas kernels for 0%

profile of v1, /device:TPU:9, one launch (start us, length us, event | category | flops | bytes accessed | tf_op | source)
XLA Modules:
  0.0 69.9 jit_solution(7125633096779454571)
XLA Ops:
  0.0 1.6 %fusion.1 = (f32[192,4]{1,0:T(8,128)S(1)}, f32[192,4]{1,0:T(8,128)}) fusion(f32[192,448]{1,0:T(8,128)} %east_ref.1), kind=kLoop, calls=%fused_computation.16 | loop fusion | bytes 12288 | tf_op jit(solution)/shard_map/slice | solution.py:302
  1.6 0.7 %slice_bitcast_fusion = (f32[1,8,448]{2,1,0:T(8,128)S(1)}, f32[1,8,448]{2,1,0:T(8,128)S(1)}) fusion(f32[192,448]{1,0:T(8,128)} %east_ref.1), kind=kLoop, calls=%fused_computation.11 | loop fusion | bytes 57344 | tf_op jit(solution)/shard_map/stack | solution.py:310
  2.3 1.7 %fusion = (f32[192,4]{1,0:T(8,128)}, f32[192,4]{1,0:T(8,128)}) fusion(f32[192,448]{1,0:T(8,128)} %north_ref.1), kind=kLoop, calls=%fused_computation.15 | loop fusion | bytes 12288 | tf_op jit(solution)/shard_map/slice | solution.py:302
  4.0 1.3 %slice_bitcast_fusion.1 = (f32[1,8,448]{2,1,0:T(8,128)S(1)}, f32[1,8,448]{2,1,0:T(8,128)}) fusion(f32[192,448]{1,0:T(8,128)} %north_ref.1), kind=kLoop, calls=%fused_computation.12 | loop fusion | bytes 57344 | tf_op jit(solution)/shard_map/stack | solution.py:310
  5.3 1.8 %slice_convert_fusion = (f32[16,192,4]{2,1,0:T(8,128)S(1)}, f32[16,192,4]{2,1,0:T(8,128)S(1)}) fusion(bf16[16,192,448]{2,1,0:T(8,128)(2,1)} %bitcast.21), kind=kLoop, calls=%fused_computation | loop fusion | flops 24576 | bytes 147456 | tf_op jit(solution)/shard_map/convert_element_type | solution.py:302
  7.1 1.7 %slice_convert_fusion.2 = (f32[16,8,448]{2,1,0:T(8,128)S(1)}, f32[16,8,448]{2,1,0:T(8,128)}) fusion(bf16[16,192,448]{2,1,0:T(8,128)(2,1)} %bitcast.22), kind=kLoop, calls=%fused_computation.7 | loop fusion | flops 114688 | bytes 688128 | tf_op jit(solution)/shard_map/convert_element_type | solution.py:310
  8.9 1.3 %copy.27 = s32[8,2]{1,0:T(8,128)} copy(s32[8,2]{0,1:T(2,128)} %param.9) | data formatting | bytes 128 | tf_op args[1]
  10.2 1.3 %reshape.15.pl_ref = s32[16]{0:T(128)} reshape(s32[8,2]{1,0:T(8,128)} %copy.27) | data formatting | bytes 128 | tf_op jit(solution)/shard_map/reshape | solution.py:334
  11.6 1.3 %copy.28 = f32[8,4]{1,0:T(8,128)} copy(f32[8,4]{0,1:T(4,128)} %param.11) | data formatting | bytes 256 | tf_op args[3]
  12.9 1.3 %reshape.16.res_ref = f32[32]{0:T(128)} reshape(f32[8,4]{1,0:T(8,128)} %copy.28) | data formatting | bytes 256 | tf_op jit(solution)/shard_map/reshape | solution.py:334
  14.2 1.6 %copy.38 = f32[192,4]{0,1:T(4,128)} copy(f32[192,4]{1,0:T(8,128)} %get-tuple-element.24) | data formatting | bytes 6144
  15.8 1.6 %copy.37 = f32[192,4]{0,1:T(4,128)} copy(f32[192,4]{1,0:T(8,128)} %get-tuple-element.22) | data formatting | bytes 6144
  17.3 1.2 %copy.31 = f32[16,192,4]{1,2,0:T(4,128)} copy(f32[16,192,4]{2,1,0:T(8,128)S(1)} %get-tuple-element.16) | data formatting | bytes 98304 | tf_op jit(solution)/shard_map/convert_element_type | solution.py:302
  18.6 0.0 copy-start
  18.6 0.0 copy-start.1
  18.6 0.9 %maximum_bitcast_fusion = f32[192,18,4]{0,2,1:T(4,128)S(1)} fusion(f32[1,192,4]{1,2,0:T(4,128)} %bitcast.24, f32[1,192,4]{1,2,0:T(4,128)} %bitcast.26, f32[16,192,4]{1,2,0:T(4,128)} %copy.31), kind=kLoop, calls=%fused_computation.9 | loop fusion | flops 27648 | bytes 110592 | tf_op jit(solution)/shard_map/transpose | solution.py:304
  19.5 0.1 copy.32
  19.6 0.1 copy.40
  19.7 1.0 %copy.39 = f32[192,4]{0,1:T(4,128)S(1)} copy(f32[192,4]{1,0:T(8,128)} %get-tuple-element.21) | data formatting | bytes 6144
  20.7 0.6 copy.35
  21.4 0.1 copy.36
  21.5 0.6 pad.14.send_l
  22.1 0.7 pad.15.send_r
  22.8 0.0 copy-done
  22.8 0.0 copy-done.1
  22.8 0.9 %select_maximum_fusion = (f32[18,8,512]{2,1,0:T(8,128)}, f32[18,8,512]{2,1,0:T(8,128)}) fusion(f32[1,8,448]{2,1,0:T(8,128)S(1)} %get-tuple-element.19, f32[1,8,448]{2,1,0:T(8,128)S(1)} %get-tuple-element.17, f32[16,8,448]{2,1,0:T(8,128)S(1)} %get-tuple-element.13, f32[1,8,448]{2,1,0:T(8,128)S(1)} %get-tuple-element.20, f32[1,8,448]{2,1,0:T(8,128)S(1)} %copy-done.1, ...), kind=kLoop, calls=%fused_computation.2 | loop fusion | flops 811008 | bytes 1105920 | tf_op jit(solution)/shard_map/concatenate | solution.py:309
  23.6 27.0 %shard_map.82 = (f32[192,128]{1,0:T(8,128)}, f32[192,128]{1,0:T(8,128)}, f32[18,8,512]{2,1,0:T(8,128)}, f32[18,8,512]{2,1,0:T(8,128)}) custom-call(f32[192,128]{1,0:T(8,128)} %pad.14.send_l, f32[192,128]{1,0:T(8,128)} %pad.15.send_r, f32[18,8,512]{2,1,0:T(8,128)} %get-tuple-element.26.top_rows, f32[18,8,512]{2,1,0:T(8,128)} %get-tuple-element.25.bot_rows), custom_call_target="tpu_custom_call" | custom-call | tf_op jit(solution)/shard_map/pallas_call | solution.py:105
  50.6 13.3 %shard_map.83 = f32[192,448]{1,0:T(8,128)} custom-call(s32[16]{0:T(128)} %reshape.15.pl_ref, s32[2]{0:T(128)} %pc_ref.1, f32[32]{0:T(128)} %reshape.16.res_ref, s32[256]{0:T(256)} %sc_ref.1, f32[4]{0:T(128)} %wav_ref.1, bf16[4,4,192,448]{3,2,1,0:T(8,128)(2,1)} %f_ref.1, f32[192,448]{1,0:T(8,128)} %north_ref.1, f32[192,448]{1,0:T(8,128)} %east_ref.1, ...), custom_call_target="tpu_custom_call" | custom-call | tf_op jit(solution)/shard_map/pallas_call | solution.py:271
  64.0 2.5 %collective-permute-start = (f32[192,448]{1,0:T(8,128)}, f32[192,448]{1,0:T(8,128)S(1)}, u32[]{:S(2)}, u32[]{:S(2)}) collective-permute-start(f32[192,448]{1,0:T(8,128)} %shard_map.83), channel_id=1, source_target_pairs={{0,128},{128,0},{1,129},{129,1},{2,130},{130,2},{3,131},{131,3},{4... | collective-permute-start | bytes 1032200 | tf_op jit(solution)/shard_map/ppermute | solution.py:336
  66.5 1.6 %collective-permute-done = f32[192,448]{1,0:T(8,128)S(1)} collective-permute-done((f32[192,448]{1,0:T(8,128)}, f32[192,448]{1,0:T(8,128)S(1)}, u32[]{:S(2)}, u32[]{:S(2)}) %collective-permute-start) | collective-permute-done | bytes 344096 | tf_op jit(solution)/shard_map/ppermute | solution.py:336
  68.1 1.8 %add.11 = f32[192,448]{1,0:T(8,128)} add(f32[192,448]{1,0:T(8,128)} %shard_map.83, f32[192,448]{1,0:T(8,128)S(1)} %collective-permute-done) | non-fusion elementwise | flops 86016 | bytes 1032192 | tf_op jit(solution)/shard_map/add | solution.py:337
  (3 shorter events, 0.1 us)
Async XLA Ops:
  18.6 4.2 %copy-start = (f32[16,8,448]{2,1,0:T(8,128)S(1)}, f32[16,8,448]{2,1,0:T(8,128)}, u32[]{:S(2)}) copy-start(f32[16,8,448]{2,1,0:T(8,128)} %get-tuple-element.14) | copy-start | bytes 688132
  18.6 4.2 %copy-start.1 = (f32[1,8,448]{2,1,0:T(8,128)S(1)}, f32[1,8,448]{2,1,0:T(8,128)}, u32[]{:S(2)}) copy-start(f32[1,8,448]{2,1,0:T(8,128)} %get-tuple-element.18) | copy-start | bytes 43012
  64.0 4.1 %collective-permute-start = (f32[192,448]{1,0:T(8,128)}, f32[192,448]{1,0:T(8,128)S(1)}, u32[]{:S(2)}, u32[]{:S(2)}) collective-permute-start(f32[192,448]{1,0:T(8,128)} %shard_map.83), channel_id=1, source_target_pairs={{0,128},{128,0},{1,129},{129,1},{2,130},{130,2},{3,131},{131,3},{4... | collective-permute-start | bytes 1032200 | tf_op jit(solution)/shard_map/ppermute | solution.py:336

commit v2 on v1

v2 whole, which is shorter than its diff:
```python
import functools

import jax
import jax.numpy as jnp
from jax import lax
from jax.experimental import pallas as pl
from jax.experimental.pallas import tpu as pltpu
from jax.sharding import PartitionSpec as P

HALO = 4
TOP = 16
COLS = 512
STRIP = 8
MESH = pl.DeviceIdType.MESH
TL, TR, BL, BR = 0, 1, 2, 3


def exchange_kernel(
    f_ref, lat_ref, lon_ref, out_l, out_r, out_a, out_b, out_c,
    pack_l, pack_r, strip_t, strip_b, tmp, tmp8, rl, rr, ra, rb, rc, send_sem, recv_sem,
):
    slots, fields, height, breadth = f_ref.shape
    count = slots * fields + 2
    nlon = lax.axis_size("lon")
    nlat = lax.axis_size("lat")
    me_lat = lax.axis_index("lat")
    me_lon = lax.axis_index("lon")
    right = lax.rem(me_lon + 1, nlon)
    left = lax.rem(me_lon + nlon - 1, nlon)
    has_up = me_lat > 0
    has_down = me_lat < nlat - 1
    up = jnp.maximum(me_lat - 1, 0)
    down = jnp.minimum(me_lat + 1, nlat - 1)

    def rows_of(a, first, size):
        if a < slots * fields:
            return f_ref[a // fields, a % fields, pl.ds(first, size), :].astype(jnp.float32)
        src = lat_ref if a == slots * fields else lon_ref
        return src[pl.ds(first, size), :]

    lane = lax.broadcasted_iota(jnp.int32, (height, 128), 1)
    quad = lane // HALO
    sub8 = lax.broadcasted_iota(jnp.int32, (STRIP, COLS), 0)
    pl_acc = jnp.zeros((height, 128), jnp.float32)
    pr_acc = jnp.zeros((height, 128), jnp.float32)
    tmp8[...] = jnp.zeros_like(tmp8)
    pending = {}
    for a in range(count):
        whole = rows_of(a, 0, height)
        tmp[:, pl.ds(0, breadth)] = whole
        head = tmp[:, pl.ds(0, 128)]
        tail = tmp[:, pl.ds(384, 128)]
        pl_acc = jnp.where(quad == a, pltpu.roll(head, (HALO * a) % 128, 1), pl_acc)
        pr_acc = jnp.where(quad == a, pltpu.roll(tail, (HALO * a - (breadth - 384 - HALO)) % 128, 1), pr_acc)
        tmp8[:, pl.ds(0, breadth)] = whole[0:STRIP]
        top = tmp8[...]
        tmp8[:, pl.ds(0, breadth)] = whole[height - STRIP : height]
        bottom = tmp8[...]
        if a % 2 == 0:
            pending = {"top": top, "bottom": bottom}
        else:
            b = a // 2
            strip_t[b] = jnp.where(sub8 < 4, pending["top"], pltpu.roll(top, 4, 0))
            strip_b[b] = jnp.where(sub8 < 4, pltpu.roll(pending["bottom"], 4, 0), bottom)
    pack_l[...] = pl_acc
    pack_r[...] = pr_acc

    barrier = pltpu.get_barrier_semaphore()
    for lon_to in (left, right):
        pl.semaphore_signal(barrier, 1, device_id={"lon": lon_to}, device_id_type=MESH)

    @pl.when(has_up)
    def _():
        for lon_to in (me_lon, left, right):
            pl.semaphore_signal(barrier, 1, device_id={"lat": up, "lon": lon_to}, device_id_type=MESH)

    @pl.when(has_down)
    def _():
        for lon_to in (me_lon, left, right):
            pl.semaphore_signal(barrier, 1, device_id={"lat": down, "lon": lon_to}, device_id_type=MESH)

    pl.semaphore_wait(barrier, 2 + 3 * has_up.astype(jnp.int32) + 3 * has_down.astype(jnp.int32))

    last8 = pl.ds(height - STRIP, STRIP)
    first8 = pl.ds(0, STRIP)
    copies = [
        (pack_r, rl, me_lat, right, None),
        (pack_l, rr, me_lat, left, None),
        (strip_t, rb, up, me_lon, "up"),
        (strip_b, ra, down, me_lon, "down"),
        (pack_r.at[last8], rc.at[TL], down, right, "down"),
        (pack_l.at[last8], rc.at[TR], down, left, "down"),
        (pack_r.at[first8], rc.at[BL], up, right, "up"),
        (pack_l.at[first8], rc.at[BR], up, left, "up"),
    ]

    def descriptor(i):
        src, dst, lat_to, lon_to, _ = copies[i]
        return pltpu.make_async_remote_copy(
            src, dst, send_sem.at[i], recv_sem.at[i], device_id={"lat": lat_to, "lon": lon_to}, device_id_type=MESH
        )

    def when(cond, fn):
        if cond is None:
            fn()
        else:
            pl.when(has_up if cond == "up" else has_down)(fn)

    for i, copy in enumerate(copies):
        when(copy[4], lambda i=i: descriptor(i).start())
    for i, copy in enumerate(copies):
        when(copy[4], lambda i=i: descriptor(i).wait_send())
        mirror = {None: None, "up": "down", "down": "up"}[copy[4]]
        when(mirror, lambda i=i: descriptor(i).wait_recv())

    @pl.when(jnp.logical_not(has_up))
    def _():
        ra[...] = jnp.zeros_like(ra)
        rc[TL] = jnp.zeros((STRIP, 128), jnp.float32)
        rc[TR] = jnp.zeros((STRIP, 128), jnp.float32)

    @pl.when(jnp.logical_not(has_down))
    def _():
        rb[...] = jnp.zeros_like(rb)
        rc[BL] = jnp.zeros((STRIP, 128), jnp.float32)
        rc[BR] = jnp.zeros((STRIP, 128), jnp.float32)

    out_l[...] = rl[...]
    out_r[...] = rr[...]
    out_a[...] = ra[...]
    out_b[...] = rb[...]
    out_c[...] = rc[...]


def exchange(wave_states, lat_faces, lon_faces):
    slots, fields, height, breadth = wave_states.shape
    count = slots * fields + 2
    vmem = pl.BlockSpec(memory_space=pltpu.VMEM)
    pack = jax.ShapeDtypeStruct((height, 128), jnp.float32)
    strip = jax.ShapeDtypeStruct((count // 2, STRIP, COLS), jnp.float32)
    corners = jax.ShapeDtypeStruct((4, STRIP, 128), jnp.float32)
    return pl.pallas_call(
        exchange_kernel,
        out_shape=[pack, pack, strip, strip, corners],
        in_specs=[vmem] * 3,
        out_specs=[vmem] * 5,
        scratch_shapes=[
            pltpu.VMEM(pack.shape, jnp.float32),
            pltpu.VMEM(pack.shape, jnp.float32),
            pltpu.VMEM(strip.shape, jnp.float32),
            pltpu.VMEM(strip.shape, jnp.float32),
            pltpu.VMEM((height, COLS), jnp.float32),
            pltpu.VMEM((STRIP, COLS), jnp.float32),
            pltpu.VMEM(pack.shape, jnp.float32),
            pltpu.VMEM(pack.shape, jnp.float32),
            pltpu.VMEM(strip.shape, jnp.float32),
            pltpu.VMEM(strip.shape, jnp.float32),
            pltpu.VMEM(corners.shape, jnp.float32),
            pltpu.SemaphoreType.DMA((8,)),
            pltpu.SemaphoreType.DMA((8,)),
        ],
        compiler_params=pltpu.CompilerParams(collective_id=0, has_side_effects=True),
    )(wave_states, lat_faces, lon_faces)


def wave_kernel(
    height,
    breadth,
    nlon,
    pl_ref,
    pc_ref,
    res_ref,
    sc_ref,
    wav_ref,
    f_ref,
    north_ref,
    east_ref,
    from_l,
    from_r,
    strip_a,
    strip_b,
    corner,
    o_ref,
    cn,
    ca,
    ce,
    cw,
    cd,
    acc,
    bufs,
    halo,
    from_a,
    from_b,
):
    s = pl.program_id(0)
    rows = cn.shape[0]
    steps = wav_ref.shape[0]
    slots = pl.num_programs(0)
    fields = f_ref.shape[1]
    lane = lax.broadcasted_iota(jnp.int32, (height, 128), 1)

    def assemble(dst, raw, a):
        dst[pl.ds(TOP, height), pl.ds(0, breadth)] = raw
        tail = dst[pl.ds(TOP, height), pl.ds(384, 128)]
        dst[pl.ds(TOP, height), pl.ds(384, 128)] = jnp.where(lane < breadth - 384, tail, halo[a])
        dst[pl.ds(TOP - STRIP, STRIP), :] = from_a[a]
        dst[pl.ds(TOP + height, STRIP), :] = from_b[a]
        dst[pl.ds(0, TOP - STRIP), :] = jnp.zeros((TOP - STRIP, COLS), jnp.float32)
        dst[pl.ds(TOP + height + STRIP, rows - TOP - height - STRIP), :] = jnp.zeros(
            (rows - TOP - height - STRIP, COLS), jnp.float32
        )

    @pl.when(s == 0)
    def _():
        fr = from_r[...]
        fl = from_l[...]
        east_gap = (lane >= breadth - 384) & (lane < breadth - 384 + HALO)
        west_gap = lane >= 128 - HALO
        sub8 = lax.broadcasted_iota(jnp.int32, (STRIP, COLS), 0)
        sub_c = lax.broadcasted_iota(jnp.int32, (STRIP, 128), 0)
        lane_c = lax.broadcasted_iota(jnp.int32, (STRIP, 128), 1)
        east_c = (lane_c >= breadth - 384) & (lane_c < breadth - 384 + HALO)
        west_c = lane_c >= 128 - HALO
        for a in range(halo.shape[0]):
            east_shift = (breadth - 384 - HALO * a) % 128
            west_shift = (128 - HALO - HALO * a) % 128
            hr = pltpu.roll(fr, east_shift, 1)
            hl = pltpu.roll(fl, west_shift, 1)
            halo[a] = jnp.where(east_gap, hr, jnp.where(west_gap, hl, jnp.float32(0.0)))
            b = a // 2
            blk = strip_a[b]
            blk = pltpu.roll(blk, 4, 0) if a % 2 == 0 else blk
            from_a[a] = jnp.where(sub8 >= 4, blk, jnp.float32(0.0))
            tail = from_a[a, :, pl.ds(384, 128)]
            low = sub_c >= 4
            tail = jnp.where(low & east_c, pltpu.roll(corner[TR], east_shift, 1), tail)
            tail = jnp.where(low & west_c, pltpu.roll(corner[TL], west_shift, 1), tail)
            from_a[a, :, pl.ds(384, 128)] = tail
            blk = strip_b[b]
            blk = blk if a % 2 == 0 else pltpu.roll(blk, 4, 0)
            from_b[a] = jnp.where(sub8 < 4, blk, jnp.float32(0.0))
            tail = from_b[a, :, pl.ds(384, 128)]
            high = sub_c < 4
            tail = jnp.where(high & east_c, pltpu.roll(corner[BR], east_shift, 1), tail)
            tail = jnp.where(high & west_c, pltpu.roll(corner[BL], west_shift, 1), tail)
            from_b[a, :, pl.ds(384, 128)] = tail
        coef_base = slots * fields
        assemble(cn, north_ref[...], coef_base)
        assemble(ce, east_ref[...], coef_base + 1)

        @pl.when(lax.axis_index("lat") == lax.axis_size("lat") - 1)
        def _():
            last = TOP + height - 8
            sub8 = lax.broadcasted_iota(jnp.int32, (8, COLS), 0)
            cn[pl.ds(last, 8), :] = jnp.where(sub8 == 7, jnp.float32(0.0), cn[pl.ds(last, 8), :])

        zero8 = jnp.zeros((8, COLS), jnp.float32)
        ca[pl.ds(8, rows - 16), :] = cn[pl.ds(7, rows - 16), :]
        ca[pl.ds(0, 8), :] = zero8
        ca[pl.ds(rows - 8, 8), :] = zero8
        cw[...] = pltpu.roll(ce[...], 1, 1)
        cd[...] = 2.0 - (cn[...] + ca[...] + ce[...] + cw[...])
        acc[...] = jnp.zeros_like(acc)

    member = lax.axis_index("pair")
    row_first = lax.axis_index("lat") * height
    col_first = lax.axis_index("lon") * breadth
    slot = member * slots + s
    act = jnp.where(s < pc_ref[member], jnp.float32(1.0), jnp.float32(0.0))

    places = []
    for comp in range(2):
        cell = sc_ref[pl_ref[slot, comp]]
        r = lax.div(cell, nlon)
        c = cell - r * nlon
        rb = r - row_first + TOP
        d = c - col_first
        d = jnp.where(d < 0, d + nlon, d)
        near = d < breadth + HALO
        wrap = d >= nlon - HALO
        cb = jnp.where(near, d, d - nlon + COLS)
        valid = (rb >= TOP - HALO) & (rb < TOP + height + HALO) & (near | wrap)
        places.append((rb, cb, valid))

    for comp in range(2):
        assemble(bufs.at[comp, 0], f_ref[0, comp].astype(jnp.float32), s * fields + comp)
        assemble(bufs.at[comp, 1], f_ref[0, 2 + comp].astype(jnp.float32), s * fields + 2 + comp)

    sub = lax.broadcasted_iota(jnp.int32, (8, COLS), 0)
    lane8 = lax.broadcasted_iota(jnp.int32, (8, COLS), 1)
    blocks = rows // 8

    for t in range(steps):
        ei, ci, ni = t % 3, (t + 1) % 3, (t + 2) % 3
        for comp in range(2):
            rb, cb, valid = places[comp]
            amp = wav_ref[t] if comp == 0 else res_ref[slot, steps - 1 - t]

            @pl.when(valid)
            def _():
                r8 = pl.multiple_of(lax.div(rb, 8) * 8, 8)
                slab = bufs[comp, ei, pl.ds(r8, 8), :]
                hit = (sub == rb - r8) & (lane8 == cb)
                bufs[comp, ei, pl.ds(r8, 8), :] = slab - jnp.where(hit, amp, jnp.float32(0.0))

        last = t == steps - 1
        first_block, end_block = (2, blocks - 2) if last else (1, blocks - 1)
        for k in range(first_block, end_block):
            r0 = 8 * k
            dd = cd[pl.ds(r0, 8), :]
            nn = cn[pl.ds(r0, 8), :]
            aa = ca[pl.ds(r0, 8), :]
            ee = ce[pl.ds(r0, 8), :]
            ww = cw[pl.ds(r0, 8), :]
            outs = []
            for comp in range(2):
                cur = bufs[comp, ci, pl.ds(r0, 8), :]
                above = bufs[comp, ci, pl.ds(r0 - 1, 8), :]
                below = bufs[comp, ci, pl.ds(r0 + 1, 8), :]
                ear = bufs[comp, ei, pl.ds(r0, 8), :]
                west = pltpu.roll(cur, 1, 1)
                east = pltpu.roll(cur, COLS - 1, 1)
                nxt = dd * cur + nn * below + aa * above + ee * east + ww * west - ear
                bufs[comp, ni, pl.ds(r0, 8), :] = nxt
                outs.append(nxt)
            if 2 <= k < blocks - 2:
                acc[pl.ds(r0 - TOP, 8), :] += (outs[0] * act) * outs[1]

    @pl.when(s == slots - 1)
    def _():
        o_ref[...] = acc[:, pl.ds(0, breadth)]


def propagate(wave_states, lat_faces, lon_faces, halos, scalars, nlon):
    slots, fields, height, breadth = wave_states.shape
    rows = height + 2 * TOP
    count = slots * fields + 2
    smem = pl.BlockSpec(memory_space=pltpu.SMEM)
    whole2 = lambda x: pl.BlockSpec(x.shape, lambda s: (0,) * x.ndim)
    return pl.pallas_call(
        functools.partial(wave_kernel, height, breadth, nlon),
        out_shape=jax.ShapeDtypeStruct((height, breadth), jnp.float32),
        grid=(slots,),
        in_specs=[smem] * 5
        + [
            pl.BlockSpec((1, fields, height, breadth), lambda s: (s, 0, 0, 0)),
            whole2(lat_faces),
            whole2(lon_faces),
        ]
        + [whole2(x) for x in halos],
        out_specs=pl.BlockSpec((height, breadth), lambda s: (0, 0)),
        scratch_shapes=[
            pltpu.VMEM((rows, COLS), jnp.float32),
            pltpu.VMEM((rows, COLS), jnp.float32),
            pltpu.VMEM((rows, COLS), jnp.float32),
            pltpu.VMEM((rows, COLS), jnp.float32),
            pltpu.VMEM((rows, COLS), jnp.float32),
            pltpu.VMEM((height, COLS), jnp.float32),
            pltpu.VMEM((2, 3, rows, COLS), jnp.float32),
            pltpu.VMEM((count, height, 128), jnp.float32),
            pltpu.VMEM((count, STRIP, COLS), jnp.float32),
            pltpu.VMEM((count, STRIP, COLS), jnp.float32),
        ],
        compiler_params=pltpu.CompilerParams(dimension_semantics=("arbitrary",)),
    )(*scalars, wave_states, lat_faces, lon_faces, *halos)


def body(
    wave_states,
    pair_list,
    pair_counts,
    residuals,
    station_cell,
    source_wavelet,
    lat_faces,
    lon_faces,
):
    height, breadth = lat_faces.shape
    nlon = breadth * lax.axis_size("lon")
    halos = exchange(wave_states, lat_faces, lon_faces)
    scalars = (pair_list, pair_counts, residuals, station_cell, source_wavelet)
    partial = propagate(wave_states, lat_faces, lon_faces, halos, scalars, nlon)
    other = lax.ppermute(partial, "pair", [(0, 1), (1, 0)])
    return partial + other


def solution(mesh):
    in_specs = (
        P("pair", None, "lat", "lon"),
        P(),
        P(),
        P(),
        P(),
        P(),
        P("lat", "lon"),
        P("lat", "lon"),
    )
    out_specs = P("lat", "lon")
    return jax.shard_map(body, mesh=mesh, in_specs=in_specs, out_specs=out_specs, check_vma=False)
```

time: 70.5 us -> 42.9 us (0.61)
  local copies, waits for them, and re-layouts: 18.3 us -> 2.68 us
  other arithmetic: 7.13 us -> 1.8 us
  Pallas kernels: 40.3 us -> 35.1 us
  starting transfers between devices: 2.55 us -> 1.57 us
    pallas_call x1, Pallas kernels: 27 us -> 21.8 us  [exchange(): pl.pallas_call(exchange_kernel, out_shape=[pack, pack, strip, strip, corn...]
    unnamed x10 -> x2, local copies, waits for them, and re-layouts: 6.88 us -> 2.68 us
    convert_element_type x2 -> x0, other arithmetic: 3.53 us -> none  [the longest x1 1.79 us: edge_columns(): fields[:, :, cols].astype(jnp.float32)]
    slice x2 -> x0, local copies, waits for them, and re-layouts: 3.27 us -> none  [the longest x1 1.68 us: edge_columns(): lat_faces[:, cols]]
    reshape x6 -> x0, local copies, waits for them, and re-layouts: 2.86 us -> none  [the longest x1 1.34 us: body(): pair_list.reshape(-1)]
    another operation x2 -> x0, local copies, waits for them, and re-layouts: 2.07 us -> none  [edge_rows(): jnp.stack([lat_faces[rows], lon_faces[rows]])]
    convert_element_type x2 -> x0, local copies, waits for them, and re-layouts: 1.87 us -> none  [edge_columns(): fields[:, :, cols].astype(jnp.float32)]
    pad x2 -> x0, local copies, waits for them, and re-layouts: 1.3 us -> none  [edge_columns(): return jnp.pad(x, ((0, 0), (0, 128 - x.shape[1])))]
where the time goes in v2:
time: 42.9 us; the launch traced here: 42.7 us
  Pallas kernels  35.1 us (82%)
  local copies, waits for them, and re-layouts  2.68 us (6%)
  other arithmetic  1.8 us (4%)
  starting transfers between devices  1.57 us (4%)
  waiting for transfers between devices  1.56 us (4%)
    pallas_call x1, Pallas kernels, exchange(): pl.pallas_call(exchange_kernel, out_shape=[pack, pack, strip, strip, corn...  21.8 us
    pallas_call x1, Pallas kernels, propagate(): pl.pallas_call(functools.partial(wave_kernel, height, breadth, nlon), out...  13.3 us
    unnamed x2, local copies, waits for them, and re-layouts  2.68 us
    add x1, other arithmetic, body(): return partial + other  1.8 us
    ppermute x1, starting transfers between devices, body(): other = lax.ppermute(partial, 'pair', [(0, 1), (1, 0)])  1.57 us
    ppermute x1, waiting for transfers between devices, body(): other = lax.ppermute(partial, 'pair', [(0, 1), (1, 0)])  1.56 us
  transfers between devices with their start and end apart: 1, of which 1 were waited for; matrix products, arithmetic and copies ran while one was open for 0% of the time, Pallas kernels for 0%

profile of v2, /device:TPU:9, one launch (start us, length us, event | category | flops | bytes accessed | tf_op | source)
XLA Modules:
  0.0 42.7 jit_solution(8834530328100195906)
XLA Ops:
  0.0 1.3 %copy.9.pl_ref = s32[8,2]{1,0:T(8,128)} copy(s32[8,2]{0,1:T(2,128)} %param.9) | data formatting | bytes 128 | tf_op args[1]
  1.3 1.3 %copy.10.res_ref = f32[8,4]{1,0:T(8,128)} copy(f32[8,4]{0,1:T(4,128)} %param.11) | data formatting | bytes 256 | tf_op args[3]
  2.7 21.8 %shard_map.82 = (f32[192,128]{1,0:T(8,128)}, f32[192,128]{1,0:T(8,128)}, f32[9,8,512]{2,1,0:T(8,128)}, f32[9,8,512]{2,1,0:T(8,128)}, f32[4,8,128]{2,1,0:T(8,128)}) custom-call(bf16[4,4,192,448]{3,2,1,0:T(8,128)(2,1)} %f_ref.3, f32[192,448]{1,0:T(8,128)} %north_ref.1, f32[192,448]{1,0:T(8,128)} %east_ref.1), custom_call_target="tpu_custom_call" | custom-call | tf_op jit(solution)/shard_map/pallas_call | solution.py:142
  24.5 13.3 %shard_map.83 = f32[192,448]{1,0:T(8,128)} custom-call(s32[8,2]{1,0:T(8,128)} %copy.9.pl_ref, s32[2]{0:T(128)} %pc_ref.1, f32[8,4]{1,0:T(8,128)} %copy.10.res_ref, s32[256]{0:T(256)} %sc_ref.1, f32[4]{0:T(128)} %wav_ref.1, bf16[4,4,192,448]{3,2,1,0:T(8,128)(2,1)} %f_ref.3, f32[192,448]{1,0:T(8,128)} %north_ref.1, f32[192,448]{1,0:T(8,128)} %east_ref.1, ...), custom_call_target="tpu_custom_call" | custom-call | tf_op jit(solution)/shard_map/pallas_call | solution.py:340
  37.8 1.6 %collective-permute-start = (f32[192,448]{1,0:T(8,128)}, f32[192,448]{1,0:T(8,128)S(1)}, u32[]{:S(2)}, u32[]{:S(2)}) collective-permute-start(f32[192,448]{1,0:T(8,128)} %shard_map.83), channel_id=1, source_target_pairs={{0,128},{128,0},{1,129},{129,1},{2,130},{130,2},{3,131},{131,3},{4... | collective-permute-start | bytes 1032200 | tf_op jit(solution)/shard_map/ppermute | solution.py:383
  39.4 1.6 %collective-permute-done = f32[192,448]{1,0:T(8,128)S(1)} collective-permute-done((f32[192,448]{1,0:T(8,128)}, f32[192,448]{1,0:T(8,128)S(1)}, u32[]{:S(2)}, u32[]{:S(2)}) %collective-permute-start) | collective-permute-done | bytes 344096 | tf_op jit(solution)/shard_map/ppermute | solution.py:383
  40.9 1.8 %add.3 = f32[192,448]{1,0:T(8,128)} add(f32[192,448]{1,0:T(8,128)} %shard_map.83, f32[192,448]{1,0:T(8,128)S(1)} %collective-permute-done) | non-fusion elementwise | flops 86016 | bytes 1032192 | tf_op jit(solution)/shard_map/add | solution.py:384
Async XLA Ops:
  37.8 3.1 %collective-permute-start = (f32[192,448]{1,0:T(8,128)}, f32[192,448]{1,0:T(8,128)S(1)}, u32[]{:S(2)}, u32[]{:S(2)}) collective-permute-start(f32[192,448]{1,0:T(8,128)} %shard_map.83), channel_id=1, source_target_pairs={{0,128},{128,0},{1,129},{129,1},{2,130},{130,2},{3,131},{131,3},{4... | collective-permute-start | bytes 1032200 | tf_op jit(solution)/shard_map/ppermute | solution.py:383

commit v3 on v2

--- a/solution.py
+++ b/solution.py
@@ -31,6 +31,20 @@
     has_down = me_lat < nlat - 1
     up = jnp.maximum(me_lat - 1, 0)
     down = jnp.minimum(me_lat + 1, nlat - 1)
+
+    barrier = pltpu.get_barrier_semaphore()
+    for lon_to in (left, right):
+        pl.semaphore_signal(barrier, 1, device_id={"lon": lon_to}, device_id_type=MESH)
+
+    @pl.when(has_up)
+    def _():
+        for lon_to in (me_lon, left, right):
+            pl.semaphore_signal(barrier, 1, device_id={"lat": up, "lon": lon_to}, device_id_type=MESH)
+
+    @pl.when(has_down)
+    def _():
+        for lon_to in (me_lon, left, right):
+            pl.semaphore_signal(barrier, 1, device_id={"lat": down, "lon": lon_to}, device_id_type=MESH)
 
     def rows_of(a, first, size):
         if a < slots * fields:
@@ -64,20 +78,6 @@
             strip_b[b] = jnp.where(sub8 < 4, pltpu.roll(pending["bottom"], 4, 0), bottom)
     pack_l[...] = pl_acc
     pack_r[...] = pr_acc
-
-    barrier = pltpu.get_barrier_semaphore()
-    for lon_to in (left, right):
-        pl.semaphore_signal(barrier, 1, device_id={"lon": lon_to}, device_id_type=MESH)
-
-    @pl.when(has_up)
-    def _():
-        for lon_to in (me_lon, left, right):
-            pl.semaphore_signal(barrier, 1, device_id={"lat": up, "lon": lon_to}, device_id_type=MESH)
-
-    @pl.when(has_down)
-    def _():
-        for lon_to in (me_lon, left, right):
-            pl.semaphore_signal(barrier, 1, device_id={"lat": down, "lon": lon_to}, device_id_type=MESH)
 
     pl.semaphore_wait(barrier, 2 + 3 * has_up.astype(jnp.int32) + 3 * has_down.astype(jnp.int32))
 
@@ -270,7 +270,7 @@
 
     places = []
     for comp in range(2):
-        cell = sc_ref[pl_ref[slot, comp]]
+        cell = sc_ref[pl_ref[comp, slot]]
         r = lax.div(cell, nlon)
         c = cell - r * nlon
         rb = r - row_first + TOP
@@ -294,7 +294,7 @@
         ei, ci, ni = t % 3, (t + 1) % 3, (t + 2) % 3
         for comp in range(2):
             rb, cb, valid = places[comp]
-            amp = wav_ref[t] if comp == 0 else res_ref[slot, steps - 1 - t]
+            amp = wav_ref[t] if comp == 0 else res_ref[steps - 1 - t, slot]
 
             @pl.when(valid)
             def _():
@@ -378,7 +378,7 @@
     height, breadth = lat_faces.shape
     nlon = breadth * lax.axis_size("lon")
     halos = exchange(wave_states, lat_faces, lon_faces)
-    scalars = (pair_list, pair_counts, residuals, station_cell, source_wavelet)
+    scalars = (pair_list.T, pair_counts, residuals.T, station_cell, source_wavelet)
     partial = propagate(wave_states, lat_faces, lon_faces, halos, scalars, nlon)
     other = lax.ppermute(partial, "pair", [(0, 1), (1, 0)])
     return partial + other

time: 42.9 us -> 39.1 us (0.911)
  local copies, waits for them, and re-layouts: 2.68 us -> 0 us
  Pallas kernels: 35.1 us -> 34.1 us
    unnamed x2 -> x0, local copies, waits for them, and re-layouts: 2.68 us -> none
    pallas_call x1, Pallas kernels: 21.8 us -> 20.7 us  [exchange(): pl.pallas_call(exchange_kernel, out_shape=[pack, pack, strip, strip, corn...]
where the time goes in v3:
time: 39.1 us; the launch traced here: 39 us
  Pallas kernels  34.1 us (87%)
  other arithmetic  1.8 us (5%)
  waiting for transfers between devices  1.56 us (4%)
  starting transfers between devices  1.55 us (4%)
    pallas_call x1, Pallas kernels, exchange(): pl.pallas_call(exchange_kernel, out_shape=[pack, pack, strip, strip, corn...  20.7 us
    pallas_call x1, Pallas kernels, propagate(): pl.pallas_call(functools.partial(wave_kernel, height, breadth, nlon), out...  13.3 us
    add x1, other arithmetic, body(): return partial + other  1.8 us
    ppermute x1, waiting for transfers between devices, body(): other = lax.ppermute(partial, 'pair', [(0, 1), (1, 0)])  1.56 us
    ppermute x1, starting transfers between devices, body(): other = lax.ppermute(partial, 'pair', [(0, 1), (1, 0)])  1.55 us
  transfers between devices with their start and end apart: 1, of which 1 were waited for; matrix products, arithmetic and copies ran while one was open for 0% of the time, Pallas kernels for 0%

profile of v3, /device:TPU:9, one launch (start us, length us, event | category | flops | bytes accessed | tf_op | source)
XLA Modules:
  0.0 39.0 jit_solution(7440235061345670717)
XLA Ops:
  0.0 20.7 %shard_map.82 = (f32[192,128]{1,0:T(8,128)}, f32[192,128]{1,0:T(8,128)}, f32[9,8,512]{2,1,0:T(8,128)}, f32[9,8,512]{2,1,0:T(8,128)}, f32[4,8,128]{2,1,0:T(8,128)}) custom-call(bf16[4,4,192,448]{3,2,1,0:T(8,128)(2,1)} %f_ref.3, f32[192,448]{1,0:T(8,128)} %north_ref.1, f32[192,448]{1,0:T(8,128)} %east_ref.1), custom_call_target="tpu_custom_call" | custom-call | tf_op jit(solution)/shard_map/pallas_call | solution.py:142
  20.7 13.3 %shard_map.83 = f32[192,448]{1,0:T(8,128)} custom-call(s32[2,8]{1,0:T(2,128)} %bitcast.3, s32[2]{0:T(128)} %pc_ref.1, f32[4,8]{1,0:T(4,128)} %bitcast.2, s32[256]{0:T(256)} %sc_ref.1, f32[4]{0:T(128)} %wav_ref.1, bf16[4,4,192,448]{3,2,1,0:T(8,128)(2,1)} %f_ref.3, f32[192,448]{1,0:T(8,128)} %north_ref.1, f32[192,448]{1,0:T(8,128)} %east_ref.1, ...), custom_call_target="tpu_custom_call" | custom-call | tf_op jit(solution)/shard_map/pallas_call | solution.py:340
  34.1 1.5 %collective-permute-start = (f32[192,448]{1,0:T(8,128)}, f32[192,448]{1,0:T(8,128)S(1)}, u32[]{:S(2)}, u32[]{:S(2)}) collective-permute-start(f32[192,448]{1,0:T(8,128)} %shard_map.83), channel_id=1, source_target_pairs={{0,128},{128,0},{1,129},{129,1},{2,130},{130,2},{3,131},{131,3},{4... | collective-permute-start | bytes 1032200 | tf_op jit(solution)/shard_map/ppermute | solution.py:383
  35.6 1.6 %collective-permute-done = f32[192,448]{1,0:T(8,128)S(1)} collective-permute-done((f32[192,448]{1,0:T(8,128)}, f32[192,448]{1,0:T(8,128)S(1)}, u32[]{:S(2)}, u32[]{:S(2)}) %collective-permute-start) | collective-permute-done | bytes 344096 | tf_op jit(solution)/shard_map/ppermute | solution.py:383
  37.2 1.8 %add.3 = f32[192,448]{1,0:T(8,128)} add(f32[192,448]{1,0:T(8,128)} %shard_map.83, f32[192,448]{1,0:T(8,128)S(1)} %collective-permute-done) | non-fusion elementwise | flops 86016 | bytes 1032192 | tf_op jit(solution)/shard_map/add | solution.py:384
Async XLA Ops:
  34.1 3.1 %collective-permute-start = (f32[192,448]{1,0:T(8,128)}, f32[192,448]{1,0:T(8,128)S(1)}, u32[]{:S(2)}, u32[]{:S(2)}) collective-permute-start(f32[192,448]{1,0:T(8,128)} %shard_map.83), channel_id=1, source_target_pairs={{0,128},{128,0},{1,129},{129,1},{2,130},{130,2},{3,131},{131,3},{4... | collective-permute-start | bytes 1032200 | tf_op jit(solution)/shard_map/ppermute | solution.py:383

commit v4 on v3

--- a/solution.py
+++ b/solution.py
@@ -17,10 +17,13 @@
 
 def exchange_kernel(
     f_ref, lat_ref, lon_ref, out_l, out_r, out_a, out_b, out_c,
-    pack_l, pack_r, strip_t, strip_b, tmp, tmp8, rl, rr, ra, rb, rc, send_sem, recv_sem,
+    pack_l, pack_r, strip_t, strip_b, tmp, tmp8,
+    send_lb, send_rb, send_lc, send_rc, send_tb, send_bb, send_tc, send_bc,
+    rlb, rrb, rlc, rrc, rab, rbb, rac, rbc, rc, send_sem, recv_sem,
 ):
     slots, fields, height, breadth = f_ref.shape
     count = slots * fields + 2
+    nfield = slots * fields
     nlon = lax.axis_size("lon")
     nlat = lax.axis_size("lat")
     me_lat = lax.axis_index("lat")
@@ -47,14 +50,15 @@
             pl.semaphore_signal(barrier, 1, device_id={"lat": down, "lon": lon_to}, device_id_type=MESH)
 
     def rows_of(a, first, size):
-        if a < slots * fields:
+        if a < nfield:
             return f_ref[a // fields, a % fields, pl.ds(first, size), :].astype(jnp.float32)
-        src = lat_ref if a == slots * fields else lon_ref
+        src = lat_ref if a == nfield else lon_ref
         return src[pl.ds(first, size), :]
 
     lane = lax.broadcasted_iota(jnp.int32, (height, 128), 1)
     quad = lane // HALO
     sub8 = lax.broadcasted_iota(jnp.int32, (STRIP, COLS), 0)
+    lane8 = lax.broadcasted_iota(jnp.int32, (STRIP, 128), 1)
     pl_acc = jnp.zeros((height, 128), jnp.float32)
     pr_acc = jnp.zeros((height, 128), jnp.float32)
     tmp8[...] = jnp.zeros_like(tmp8)
@@ -79,15 +83,39 @@
     pack_l[...] = pl_acc
     pack_r[...] = pr_acc
 
+    coef_lane = HALO * nfield
+    width = 2 * HALO
+    per_row = 128 // width
+    send_lb[...] = pl_acc.astype(jnp.bfloat16)
+    send_rb[...] = pr_acc.astype(jnp.bfloat16)
+    for src, dst in ((pl_acc, send_lc), (pr_acc, send_rc)):
+        for h in range(dst.shape[0] // STRIP):
+            packed = jnp.zeros((STRIP, 128), jnp.float32)
+            for g in range(per_row):
+                i = h * per_row + g
+                if i * STRIP >= height:
+                    break
+                blk = src[i * STRIP : (i + 1) * STRIP]
+                packed = jnp.where(lane8 // width == g, pltpu.roll(blk, (width * g - coef_lane) % 128, 1), packed)
+            dst[pl.ds(h * STRIP, STRIP), :] = packed
+    for src, dst_b, dst_c in ((strip_t, send_tb, send_tc), (strip_b, send_bb, send_bc)):
+        for j in range(dst_b.shape[0]):
+            dst_b[j] = jnp.concatenate([src[2 * j], src[2 * j + 1]], axis=0).astype(jnp.bfloat16)
+        dst_c[...] = src[nfield // 2]
+
     pl.semaphore_wait(barrier, 2 + 3 * has_up.astype(jnp.int32) + 3 * has_down.astype(jnp.int32))
 
     last8 = pl.ds(height - STRIP, STRIP)
     first8 = pl.ds(0, STRIP)
     copies = [
-        (pack_r, rl, me_lat, right, None),
-        (pack_l, rr, me_lat, left, None),
-        (strip_t, rb, up, me_lon, "up"),
-        (strip_b, ra, down, me_lon, "down"),
+        (send_rb, rlb, me_lat, right, None),
+        (send_rc, rlc, me_lat, right, None),
+        (send_lb, rrb, me_lat, left, None),
+        (send_lc, rrc, me_lat, left, None),
+        (send_tb, rbb, up, me_lon, "up"),
+        (send_tc, rbc, up, me_lon, "up"),
+        (send_bb, rab, down, me_lon, "down"),
+        (send_bc, rac, down, me_lon, "down"),
         (pack_r.at[last8], rc.at[TL], down, right, "down"),
         (pack_l.at[last8], rc.at[TR], down, left, "down"),
         (pack_r.at[first8], rc.at[BL], up, right, "up"),
@@ -115,30 +143,50 @@
 
     @pl.when(jnp.logical_not(has_up))
     def _():
-        ra[...] = jnp.zeros_like(ra)
+        rab[...] = jnp.zeros_like(rab)
+        rac[...] = jnp.zeros_like(rac)
         rc[TL] = jnp.zeros((STRIP, 128), jnp.float32)
         rc[TR] = jnp.zeros((STRIP, 128), jnp.float32)
 
     @pl.when(jnp.logical_not(has_down))
     def _():
-        rb[...] = jnp.zeros_like(rb)
+        rbb[...] = jnp.zeros_like(rbb)
+        rbc[...] = jnp.zeros_like(rbc)
         rc[BL] = jnp.zeros((STRIP, 128), jnp.float32)
         rc[BR] = jnp.zeros((STRIP, 128), jnp.float32)
 
-    out_l[...] = rl[...]
-    out_r[...] = rr[...]
-    out_a[...] = ra[...]
-    out_b[...] = rb[...]
+    for src_b, src_c, dst in ((rlb, rlc, out_l), (rrb, rrc, out_r)):
+        fields_part = src_b[...].astype(jnp.float32)
+        for i in range(height // STRIP):
+            h, g = divmod(i, per_row)
+            blk_c = pltpu.roll(src_c[pl.ds(h * STRIP, STRIP), :], (coef_lane - width * g) % 128, 1)
+            blk_f = fields_part[i * STRIP : (i + 1) * STRIP]
+            dst[pl.ds(i * STRIP, STRIP), :] = jnp.where(
+                lane8 < coef_lane, blk_f, jnp.where(lane8 < coef_lane + width, blk_c, jnp.float32(0.0))
+            )
+    for src_b, src_c, dst in ((rab, rac, out_a), (rbb, rbc, out_b)):
+        for j in range(src_b.shape[0]):
+            both = src_b[j].astype(jnp.float32)
+            dst[2 * j] = both[0:STRIP]
+            dst[2 * j + 1] = both[STRIP : 2 * STRIP]
+        dst[nfield // 2] = src_c[...]
     out_c[...] = rc[...]
 
 
 def exchange(wave_states, lat_faces, lon_faces):
     slots, fields, height, breadth = wave_states.shape
     count = slots * fields + 2
+    nfield = slots * fields
     vmem = pl.BlockSpec(memory_space=pltpu.VMEM)
     pack = jax.ShapeDtypeStruct((height, 128), jnp.float32)
     strip = jax.ShapeDtypeStruct((count // 2, STRIP, COLS), jnp.float32)
     corners = jax.ShapeDtypeStruct((4, STRIP, 128), jnp.float32)
+    per_row = 128 // (2 * HALO)
+    coef_rows = STRIP * ((height // STRIP + per_row - 1) // per_row)
+    packed_b = pltpu.VMEM((height, 128), jnp.bfloat16)
+    packed_c = pltpu.VMEM((coef_rows, 128), jnp.float32)
+    strip_b16 = pltpu.VMEM((nfield // 4, 2 * STRIP, COLS), jnp.bfloat16)
+    strip_c = pltpu.VMEM((STRIP, COLS), jnp.float32)
     return pl.pallas_call(
         exchange_kernel,
         out_shape=[pack, pack, strip, strip, corners],
@@ -151,13 +199,12 @@
             pltpu.VMEM(strip.shape, jnp.float32),
             pltpu.VMEM((height, COLS), jnp.float32),
             pltpu.VMEM((STRIP, COLS), jnp.float32),
-            pltpu.VMEM(pack.shape, jnp.float32),
-            pltpu.VMEM(pack.shape, jnp.float32),
-            pltpu.VMEM(strip.shape, jnp.float32),
-            pltpu.VMEM(strip.shape, jnp.float32),
+        ]
+        + [packed_b, packed_b, packed_c, packed_c, strip_b16, strip_b16, strip_c, strip_c] * 2
+        + [
             pltpu.VMEM(corners.shape, jnp.float32),
-            pltpu.SemaphoreType.DMA((8,)),
-            pltpu.SemaphoreType.DMA((8,)),
+            pltpu.SemaphoreType.DMA((12,)),
+            pltpu.SemaphoreType.DMA((12,)),
         ],
         compiler_params=pltpu.CompilerParams(collective_id=0, has_side_effects=True),
     )(wave_states, lat_faces, lon_faces)

time: 39.1 us -> 35.7 us (0.913)
  the two profiles are of different devices: /device:TPU:9 before, /device:TPU:1 now
where the time goes in v4:
time: 35.7 us; the launch traced here: 35.5 us
  Pallas kernels  29.4 us (82%)
  starting transfers between devices  2.8 us (8%)
  other arithmetic  1.8 us (5%)
  waiting for transfers between devices  1.56 us (4%)
    pallas_call x1, Pallas kernels, exchange(): pl.pallas_call(exchange_kernel, out_shape=[pack, pack, strip, strip, corn...  16 us
    pallas_call x1, Pallas kernels, propagate(): pl.pallas_call(functools.partial(wave_kernel, height, breadth, nlon), out...  13.3 us
    ppermute x1, starting transfers between devices, body(): other = lax.ppermute(partial, 'pair', [(0, 1), (1, 0)])  2.8 us
    add x1, other arithmetic, body(): return partial + other  1.8 us
    ppermute x1, waiting for transfers between devices, body(): other = lax.ppermute(partial, 'pair', [(0, 1), (1, 0)])  1.56 us
  transfers between devices with their start and end apart: 1, of which 1 were waited for; matrix products, arithmetic and copies ran while one was open for 0% of the time, Pallas kernels for 0%

profile of v4, /device:TPU:1, one launch (start us, length us, event | category | flops | bytes accessed | tf_op | source)
XLA Modules:
  0.0 35.5 jit_solution(1890840913127520388)
XLA Ops:
  0.0 16.0 %shard_map.82 = (f32[192,128]{1,0:T(8,128)}, f32[192,128]{1,0:T(8,128)}, f32[9,8,512]{2,1,0:T(8,128)}, f32[9,8,512]{2,1,0:T(8,128)}, f32[4,8,128]{2,1,0:T(8,128)}) custom-call(bf16[4,4,192,448]{3,2,1,0:T(8,128)(2,1)} %f_ref.3, f32[192,448]{1,0:T(8,128)} %north_ref.1, f32[192,448]{1,0:T(8,128)} %east_ref.1), custom_call_target="tpu_custom_call" | custom-call | tf_op jit(solution)/shard_map/pallas_call | solution.py:190
  16.0 13.3 %shard_map.83 = f32[192,448]{1,0:T(8,128)} custom-call(s32[2,8]{1,0:T(2,128)} %bitcast.3, s32[2]{0:T(128)} %pc_ref.1, f32[4,8]{1,0:T(4,128)} %bitcast.2, s32[256]{0:T(256)} %sc_ref.1, f32[4]{0:T(128)} %wav_ref.1, bf16[4,4,192,448]{3,2,1,0:T(8,128)(2,1)} %f_ref.3, f32[192,448]{1,0:T(8,128)} %north_ref.1, f32[192,448]{1,0:T(8,128)} %east_ref.1, ...), custom_call_target="tpu_custom_call" | custom-call | tf_op jit(solution)/shard_map/pallas_call | solution.py:387
  29.4 2.8 %collective-permute-start = (f32[192,448]{1,0:T(8,128)}, f32[192,448]{1,0:T(8,128)S(1)}, u32[]{:S(2)}, u32[]{:S(2)}) collective-permute-start(f32[192,448]{1,0:T(8,128)} %shard_map.83), channel_id=1, source_target_pairs={{0,128},{128,0},{1,129},{129,1},{2,130},{130,2},{3,131},{131,3},{4... | collective-permute-start | bytes 1032200 | tf_op jit(solution)/shard_map/ppermute | solution.py:430
  32.2 1.6 %collective-permute-done = f32[192,448]{1,0:T(8,128)S(1)} collective-permute-done((f32[192,448]{1,0:T(8,128)}, f32[192,448]{1,0:T(8,128)S(1)}, u32[]{:S(2)}, u32[]{:S(2)}) %collective-permute-start) | collective-permute-done | bytes 344096 | tf_op jit(solution)/shard_map/ppermute | solution.py:430
  33.7 1.8 %add.3 = f32[192,448]{1,0:T(8,128)} add(f32[192,448]{1,0:T(8,128)} %shard_map.83, f32[192,448]{1,0:T(8,128)S(1)} %collective-permute-done) | non-fusion elementwise | flops 86016 | bytes 1032192 | tf_op jit(solution)/shard_map/add | solution.py:431
Async XLA Ops:
  29.4 4.4 %collective-permute-start = (f32[192,448]{1,0:T(8,128)}, f32[192,448]{1,0:T(8,128)S(1)}, u32[]{:S(2)}, u32[]{:S(2)}) collective-permute-start(f32[192,448]{1,0:T(8,128)} %shard_map.83), channel_id=1, source_target_pairs={{0,128},{128,0},{1,129},{129,1},{2,130},{130,2},{3,131},{131,3},{4... | collective-permute-start | bytes 1032200 | tf_op jit(solution)/shard_map/ppermute | solution.py:430

commit v5 on v0

v5 whole, which is shorter than its diff:
```python
import functools

import jax
import jax.numpy as jnp
from jax import lax
from jax.experimental import pallas as pl
from jax.experimental.pallas import tpu as pltpu
from jax.sharding import PartitionSpec as P

HALO = 4
TOP = 16
COLS = 512
STRIP = 8
MESH = pl.DeviceIdType.MESH
TL, TR, BL, BR = 0, 1, 2, 3


def fused_kernel(
    nlon_cells,
    pl_ref, pc_ref, res_ref, sc_ref, wav_ref,
    f_ref, lat_ref, lon_ref,
    o_ref,
    X, work, ca, cw, cd, acc, pacc,
    pack_l, pack_r,
    send_lb, send_rb, send_lc, send_rc, send_tb, send_bb, send_tc, send_bc,
    rlb, rrb, rlc, rrc, rab, rbb, rac, rbc, rc,
    send_sem, recv_sem,
):
    slots, fields, height, breadth = f_ref.shape
    nfield = slots * fields
    count = nfield + 2
    rows = X.shape[1]
    blocks = rows // 8
    steps = wav_ref.shape[0]
    nlon = lax.axis_size("lon")
    nlat = lax.axis_size("lat")
    me_lat = lax.axis_index("lat")
    me_lon = lax.axis_index("lon")
    member = lax.axis_index("pair")
    partner = 1 - member
    right = lax.rem(me_lon + 1, nlon)
    left = lax.rem(me_lon + nlon - 1, nlon)
    has_up = me_lat > 0
    has_down = me_lat < nlat - 1
    up = jnp.maximum(me_lat - 1, 0)
    down = jnp.minimum(me_lat + 1, nlat - 1)
    cn = X.at[nfield]
    ce = X.at[nfield + 1]

    barrier = pltpu.get_barrier_semaphore()
    pl.semaphore_signal(barrier, 1, device_id={"pair": partner}, device_id_type=MESH)
    for lon_to in (left, right):
        pl.semaphore_signal(barrier, 1, device_id={"lon": lon_to}, device_id_type=MESH)

    @pl.when(has_up)
    def _():
        for lon_to in (me_lon, left, right):
            pl.semaphore_signal(barrier, 1, device_id={"lat": up, "lon": lon_to}, device_id_type=MESH)

    @pl.when(has_down)
    def _():
        for lon_to in (me_lon, left, right):
            pl.semaphore_signal(barrier, 1, device_id={"lat": down, "lon": lon_to}, device_id_type=MESH)

    lane = lax.broadcasted_iota(jnp.int32, (height, 128), 1)
    quad = lane // HALO
    sub8 = lax.broadcasted_iota(jnp.int32, (STRIP, COLS), 0)
    lane8 = lax.broadcasted_iota(jnp.int32, (STRIP, 128), 1)
    sub_c = lax.broadcasted_iota(jnp.int32, (STRIP, 128), 0)
    lane_w = lax.broadcasted_iota(jnp.int32, (STRIP, COLS), 1)
    zero_rows = jnp.zeros((TOP, COLS), jnp.float32)

    for a in range(count):
        if a < nfield:
            raw = f_ref[a // fields, a % fields].astype(jnp.float32)
        else:
            raw = (lat_ref if a == nfield else lon_ref)[...]
        X[a, pl.ds(TOP, height), pl.ds(0, breadth)] = raw
        tail = X[a, pl.ds(TOP, height), pl.ds(384, 128)]
        X[a, pl.ds(TOP, height), pl.ds(384, 128)] = jnp.where(lane < breadth - 384, tail, jnp.float32(0.0))
        X[a, pl.ds(0, TOP), :] = zero_rows
        X[a, pl.ds(TOP + height, rows - TOP - height), :] = zero_rows

    @pl.when(me_lat == nlat - 1)
    def _():
        last = TOP + height - 8
        cn[pl.ds(last, 8), :] = jnp.where(sub8 == 7, jnp.float32(0.0), cn[pl.ds(last, 8), :])

    pl_acc = jnp.zeros((height, 128), jnp.float32)
    pr_acc = jnp.zeros((height, 128), jnp.float32)
    for a in range(count):
        head = X[a, pl.ds(TOP, height), pl.ds(0, 128)]
        tail = X[a, pl.ds(TOP, height), pl.ds(384, 128)]
        pl_acc = jnp.where(quad == a, pltpu.roll(head, (HALO * a) % 128, 1), pl_acc)
        pr_acc = jnp.where(quad == a, pltpu.roll(tail, (HALO * a - (breadth - 384 - HALO)) % 128, 1), pr_acc)
    pack_l[...] = pl_acc
    pack_r[...] = pr_acc

    coef_lane = HALO * nfield
    width = 2 * HALO
    per_row = 128 // width
    send_lb[...] = pl_acc.astype(jnp.bfloat16)
    send_rb[...] = pr_acc.astype(jnp.bfloat16)
    for src, dst in ((pl_acc, send_lc), (pr_acc, send_rc)):
        for h in range(dst.shape[0] // STRIP):
            packed = jnp.zeros((STRIP, 128), jnp.float32)
            for g in range(per_row):
                i = h * per_row + g
                if i * STRIP >= height:
                    break
                blk = src[i * STRIP : (i + 1) * STRIP]
                packed = jnp.where(lane8 // width == g, pltpu.roll(blk, (width * g - coef_lane) % 128, 1), packed)
            dst[pl.ds(h * STRIP, STRIP), :] = packed

    def strip_pair(a, first, keep_low):
        lo = X[a, pl.ds(first, STRIP), :]
        hi = X[a + 1, pl.ds(first, STRIP), :]
        if keep_low:
            return jnp.where(sub8 < 4, lo, pltpu.roll(hi, 4, 0))
        return jnp.where(sub8 < 4, pltpu.roll(lo, 4, 0), hi)

    for dst_b, dst_c, first, keep_low in (
        (send_tb, send_tc, TOP, True),
        (send_bb, send_bc, TOP + height - STRIP, False),
    ):
        for j in range(dst_b.shape[0]):
            both = [strip_pair(4 * j, first, keep_low), strip_pair(4 * j + 2, first, keep_low)]
            dst_b[j] = jnp.concatenate(both, axis=0).astype(jnp.bfloat16)
        dst_c[...] = strip_pair(nfield, first, keep_low)

    pl.semaphore_wait(barrier, 3 + 3 * has_up.astype(jnp.int32) + 3 * has_down.astype(jnp.int32))

    last8 = pl.ds(height - STRIP, STRIP)
    first8 = pl.ds(0, STRIP)
    copies = [
        (send_rb, rlb, me_lat, right, None),
        (send_rc, rlc, me_lat, right, None),
        (send_lb, rrb, me_lat, left, None),
        (send_lc, rrc, me_lat, left, None),
        (send_tb, rbb, up, me_lon, "up"),
        (send_tc, rbc, up, me_lon, "up"),
        (send_bb, rab, down, me_lon, "down"),
        (send_bc, rac, down, me_lon, "down"),
        (pack_r.at[last8], rc.at[TL], down, right, "down"),
        (pack_l.at[last8], rc.at[TR], down, left, "down"),
        (pack_r.at[first8], rc.at[BL], up, right, "up"),
        (pack_l.at[first8], rc.at[BR], up, left, "up"),
    ]

    def descriptor(i):
        src, dst, lat_to, lon_to, _ = copies[i]
        return pltpu.make_async_remote_copy(
            src, dst, send_sem.at[i], recv_sem.at[i], device_id={"lat": lat_to, "lon": lon_to}, device_id_type=MESH
        )

    def when(cond, fn):
        if cond is None:
            fn()
        else:
            pl.when(has_up if cond == "up" else has_down)(fn)

    def finish(i):
        cond = copies[i][4]
        when(cond, lambda: descriptor(i).wait_send())
        mirror = {None: None, "up": "down", "down": "up"}[cond]
        when(mirror, lambda: descriptor(i).wait_recv())

    for i, copy in enumerate(copies):
        when(copy[4], lambda i=i: descriptor(i).start())

    for i in range(4):
        finish(i)
    east_gap = (lane >= breadth - 384) & (lane < breadth - 384 + HALO)
    west_gap = lane >= 128 - HALO
    unpacked = []
    for src_b, src_c in ((rlb, rlc), (rrb, rrc)):
        fields_part = src_b[...].astype(jnp.float32)
        parts = []
        for i in range(height // STRIP):
            h, g = divmod(i, per_row)
            blk_c = pltpu.roll(src_c[pl.ds(h * STRIP, STRIP), :], (coef_lane - width * g) % 128, 1)
            blk_f = fields_part[i * STRIP : (i + 1) * STRIP]
            parts.append(jnp.where(lane8 < coef_lane, blk_f, blk_c))
        unpacked.append(jnp.concatenate(parts, axis=0))
    from_l, from_r = unpacked
    for a in range(count):
        east_shift = (breadth - 384 - HALO * a) % 128
        west_shift = (128 - HALO - HALO * a) % 128
        tail = X[a, pl.ds(TOP, height), pl.ds(384, 128)]
        tail = jnp.where(east_gap, pltpu.roll(from_r, east_shift, 1), tail)
        tail = jnp.where(west_gap, pltpu.roll(from_l, west_shift, 1), tail)
        X[a, pl.ds(TOP, height), pl.ds(384, 128)] = tail

    def derive(first, size):
        ca[pl.ds(first, size), :] = cn[pl.ds(first - 1, size), :]
        cw[pl.ds(first, size), :] = pltpu.roll(ce[pl.ds(first, size), :], 1, 1)
        cd[pl.ds(first, size), :] = 2.0 - (
            cn[pl.ds(first, size), :] + ca[pl.ds(first, size), :] + ce[pl.ds(first, size), :] + cw[pl.ds(first, size), :]
        )

    derive(8, rows - 16)
    acc[...] = jnp.zeros_like(acc)

    def slot_places(s):
        slot = member * slots + s
        act = jnp.where(s < pc_ref[member], jnp.float32(1.0), jnp.float32(0.0))
        row_first = me_lat * height
        col_first = me_lon * breadth
        places = []
        for comp in range(2):
            cell = sc_ref[pl_ref[comp, slot]]
            r = lax.div(cell, nlon_cells)
            c = cell - r * nlon_cells
            rb = r - row_first + TOP
            d = c - col_first
            d = jnp.where(d < 0, d + nlon_cells, d)
            near = d < breadth + HALO
            wrap = d >= nlon_cells - HALO
            cb = jnp.where(near, d, d - nlon_cells + COLS)
            valid = (rb >= TOP - HALO) & (rb < TOP + height + HALO) & (near | wrap)
            hit = (sub8 == lax.rem(jnp.maximum(rb, 0), 8)) & (lane_w == cb)
            amps = [wav_ref[t] if comp == 0 else res_ref[steps - 1 - t, slot] for t in range(steps)]
            places.append((rb, valid, hit, amps))
        return act, places

    def run_blocks(s, t, block_list, act, places):
        bufs = [(X.at[s * fields + comp], X.at[s * fields + 2 + comp], work.at[s, comp]) for comp in range(2)]
        ei, ci, ni = t % 3, (t + 1) % 3, (t + 2) % 3
        for k in block_list:
            r0 = 8 * k
            dd = cd[pl.ds(r0, 8), :]
            nn = cn[pl.ds(r0, 8), :]
            aa = ca[pl.ds(r0, 8), :]
            ee = ce[pl.ds(r0, 8), :]
            ww = cw[pl.ds(r0, 8), :]
            outs = []
            for comp in range(2):
                rb, valid, hit, amps = places[comp]
                amp = jnp.where(valid & (rb >= r0) & (rb < r0 + 8), amps[t], jnp.float32(0.0))
                cur_ref, ear_ref, nxt_ref = bufs[comp][ci], bufs[comp][ei], bufs[comp][ni]
                cur = cur_ref[pl.ds(r0, 8), :]
                above = cur_ref[pl.ds(r0 - 1, 8), :]
                below = cur_ref[pl.ds(r0 + 1, 8), :]
                ear = ear_ref[pl.ds(r0, 8), :]
                west = pltpu.roll(cur, 1, 1)
                east = pltpu.roll(cur, COLS - 1, 1)
                nxt = dd * cur + nn * below + aa * above + ee * east + ww * west - ear
                nxt = nxt + jnp.where(hit, amp, jnp.float32(0.0))
                nxt_ref[pl.ds(r0, 8), :] = nxt
                outs.append(nxt)
            if 2 <= k < blocks - 2:
                acc[pl.ds(r0 - TOP, 8), :] += (outs[0] * act) * outs[1]

    def phase(ranges):
        def body(s, carry):
            act, places = slot_places(s)
            for t in range(steps):
                run_blocks(s, t, ranges(t), act, places)
            return carry

        lax.fori_loop(0, slots, body, 0)

    inner = lambda t: list(range(3 + t, blocks - 3 - t))
    phase(inner)

    for i in range(4, len(copies)):
        finish(i)

    @pl.when(jnp.logical_not(has_up))
    def _():
        rab[...] = jnp.zeros_like(rab)
        rac[...] = jnp.zeros_like(rac)
        rc[TL] = jnp.zeros((STRIP, 128), jnp.float32)
        rc[TR] = jnp.zeros((STRIP, 128), jnp.float32)

    @pl.when(jnp.logical_not(has_down))
    def _():
        rbb[...] = jnp.zeros_like(rbb)
        rbc[...] = jnp.zeros_like(rbc)
        rc[BL] = jnp.zeros((STRIP, 128), jnp.float32)
        rc[BR] = jnp.zeros((STRIP, 128), jnp.float32)

    east_c = (lane8 >= breadth - 384) & (lane8 < breadth - 384 + HALO)
    west_c = lane8 >= 128 - HALO
    for src_b, src_c, first, low_half, (c_east, c_west) in (
        (rab, rac, TOP - STRIP, False, (TR, TL)),
        (rbb, rbc, TOP + height, True, (BR, BL)),
    ):
        for a in range(count):
            b = a // 2
            if a < nfield:
                both = src_b[b // 2].astype(jnp.float32)
                blk = both[STRIP * (b % 2) : STRIP * (b % 2 + 1)]
            else:
                blk = src_c[...]
            even = a % 2 == 0
            if low_half:
                blk = blk if even else pltpu.roll(blk, 4, 0)
                blk = jnp.where(sub8 < 4, blk, jnp.float32(0.0))
                band = sub_c < 4
            else:
                blk = pltpu.roll(blk, 4, 0) if even else blk
                blk = jnp.where(sub8 >= 4, blk, jnp.float32(0.0))
                band = sub_c >= 4
            X[a, pl.ds(first, STRIP), :] = blk
            east_shift = (breadth - 384 - HALO * a) % 128
            west_shift = (128 - HALO - HALO * a) % 128
            tail = X[a, pl.ds(first, STRIP), pl.ds(384, 128)]
            tail = jnp.where(band & east_c, pltpu.roll(rc[c_east], east_shift, 1), tail)
            tail = jnp.where(band & west_c, pltpu.roll(rc[c_west], west_shift, 1), tail)
            X[a, pl.ds(first, STRIP), pl.ds(384, 128)] = tail

    derive(8, 24)
    derive(rows - 32, 24)

    def outer(t):
        if t < steps - 1:
            return list(range(1, 3 + t)) + list(range(blocks - 3 - t, blocks - 1))
        return list(range(2, 3 + t)) + list(range(blocks - 3 - t, blocks - 2))

    phase(outer)

    to_partner = pltpu.make_async_remote_copy(
        acc, pacc, send_sem.at[len(copies)], recv_sem.at[len(copies)], device_id={"pair": partner}, device_id_type=MESH
    )
    to_partner.start()
    to_partner.wait()
    o_ref[...] = (acc[...] + pacc[...])[:, 0:breadth]


def fused(wave_states, lat_faces, lon_faces, scalars, nlon_cells):
    slots, fields, height, breadth = wave_states.shape
    nfield = slots * fields
    count = nfield + 2
    rows = height + 2 * TOP
    smem = pl.BlockSpec(memory_space=pltpu.SMEM)
    vmem = pl.BlockSpec(memory_space=pltpu.VMEM)
    per_row = 128 // (2 * HALO)
    coef_rows = STRIP * ((height // STRIP + per_row - 1) // per_row)
    packed_b = pltpu.VMEM((height, 128), jnp.bfloat16)
    packed_c = pltpu.VMEM((coef_rows, 128), jnp.float32)
    strip_b16 = pltpu.VMEM((nfield // 4, 2 * STRIP, COLS), jnp.bfloat16)
    strip_c = pltpu.VMEM((STRIP, COLS), jnp.float32)
    plane = pltpu.VMEM((rows, COLS), jnp.float32)
    return pl.pallas_call(
        functools.partial(fused_kernel, nlon_cells),
        out_shape=jax.ShapeDtypeStruct((height, breadth), jnp.float32),
        in_specs=[smem] * 5 + [vmem] * 3,
        out_specs=vmem,
        scratch_shapes=[
            pltpu.VMEM((count, rows, COLS), jnp.float32),
            pltpu.VMEM((slots, 2, rows, COLS), jnp.float32),
            plane,
            plane,
            plane,
            pltpu.VMEM((height, COLS), jnp.float32),
            pltpu.VMEM((height, COLS), jnp.float32),
            pltpu.VMEM((height, 128), jnp.float32),
            pltpu.VMEM((height, 128), jnp.float32),
        ]
        + [packed_b, packed_b, packed_c, packed_c, strip_b16, strip_b16, strip_c, strip_c] * 2
        + [
            pltpu.VMEM((4, STRIP, 128), jnp.float32),
            pltpu.SemaphoreType.DMA((13,)),
            pltpu.SemaphoreType.DMA((13,)),
        ],
        compiler_params=pltpu.CompilerParams(collective_id=0, has_side_effects=True, vmem_limit_bytes=60 * 1024 * 1024),
    )(*scalars, wave_states, lat_faces, lon_faces)


def body(
    wave_states,
    pair_list,
    pair_counts,
    residuals,
    station_cell,
    source_wavelet,
    lat_faces,
    lon_faces,
):
    height, breadth = lat_faces.shape
    nlon_cells = breadth * lax.axis_size("lon")
    scalars = (pair_list.T, pair_counts, residuals.T, station_cell, source_wavelet)
    return fused(wave_states, lat_faces, lon_faces, scalars, nlon_cells)


def solution(mesh):
    in_specs = (
        P("pair", None, "lat", "lon"),
        P(),
        P(),
        P(),
        P(),
        P(),
        P("lat", "lon"),
        P("lat", "lon"),
    )
    out_specs = P("lat", "lon")
    return jax.shard_map(body, mesh=mesh, in_specs=in_specs, out_specs=out_specs, check_vma=False)
```

time: 133 us -> 30.5 us (0.23)
  other arithmetic: 51.1 us -> 0 us
  starting transfers between devices: 30.5 us -> 0 us
  Pallas kernels: 0 us -> 28.6 us
  local copies, waits for them, and re-layouts: 26.6 us -> 1.77 us
  waiting for transfers between devices: 13.9 us -> 0 us
  blocking collectives: 9.71 us -> 0 us
    ppermute x12 -> x0, starting transfers between devices: 30.5 us -> none  [the longest x6 15.8 us: extended(): lax.ppermute(lax.slice_in_dim(block, block.shape[dim] - width, None, axis...]
    pallas_call x0 -> x1, Pallas kernels: none -> 28.6 us  [fused(): pl.pallas_call(functools.partial(fused_kernel, nlon_cells), out_shape=jax...]
    add x4 -> x0, other arithmetic: 24.8 us -> none  [the longest x3 24.6 us: advance(): return 2.0 * centre - earlier + change + source]
    ppermute x12 -> x0, waiting for transfers between devices: 13.9 us -> none  [the longest x6 13.9 us: extended(): lax.ppermute(lax.slice_in_dim(block, 0, width, axis=dim), axis, backward)]
    all_to_all x1 -> x0, blocking collectives: 9.71 us -> none  [copy_for_each(): lax.all_to_all(jnp.broadcast_to(x[None], (devices, *x.shape)), axis, 0, 0...]
    slice x5 -> x0, other arithmetic: 9.49 us -> none  [the longest x4 5.65 us: extended(): lax.slice_in_dim(block, block.shape[dim] - width, None, axis=dim)]
    slice x8 -> x0, local copies, waits for them, and re-layouts: 9.37 us -> none  [the longest x4 4.66 us: extended(): lax.slice_in_dim(block, block.shape[dim] - width, None, axis=dim)]
    concatenate x2 -> x0, other arithmetic: 8.46 us -> none  [extended(): block = jnp.concatenate([low, block, high], axis=dim)]
  transfers between devices with their start and end apart: 12 -> 0, of which waited for: 3 -> 0; matrix products, arithmetic and copies ran while one was open for 15% -> 0% of each run, Pallas kernels for 0% -> 0%
where the time goes in v5:
time: 30.5 us; the launch traced here: 30.4 us
  Pallas kernels  28.6 us (94%)
  local copies, waits for them, and re-layouts  1.77 us (6%)
    pallas_call x1, Pallas kernels, fused(): pl.pallas_call(functools.partial(fused_kernel, nlon_cells), out_shape=jax...  28.6 us
    unnamed x1, local copies, waits for them, and re-layouts  1.77 us

profile of v5, /device:TPU:1, one launch (start us, length us, event | category | flops | bytes accessed | tf_op | source)
XLA Modules:
  0.0 30.4 jit_solution(14714648121138783920)
XLA Ops:
  0.0 28.6 %shard_map.82 = f32[192,448]{1,0:T(8,128)} custom-call(s32[2,8]{1,0:T(2,128)} %bitcast.3, s32[2]{0:T(128)} %pc_ref.1, f32[4,8]{1,0:T(4,128)} %bitcast.2, s32[256]{0:T(256)} %sc_ref.1, f32[4]{0:T(128)} %wav_ref.1, bf16[4,4,192,448]{3,2,1,0:T(8,128)(2,1)} %f_ref.1, f32[192,448]{1,0:T(8,128)} %lat_ref.1, f32[192,448]{1,0:T(8,128)} %lon_ref.1), custom_call_target="tpu_custom_call" | custom-call | tf_op jit(solution)/shard_map/pallas_call | solution.py:345
  28.6 1.8 %copy.10 = f32[192,448]{1,0:T(8,128)} copy(f32[192,448]{1,0:T(8,128)} %shard_map.82) | data formatting | bytes 688128

commit v6 on v5

--- a/solution.py
+++ b/solution.py
@@ -18,8 +18,9 @@
 def fused_kernel(
     nlon_cells,
     pl_ref, pc_ref, res_ref, sc_ref, wav_ref,
-    f_ref, lat_ref, lon_ref,
+    f_hbm, lat_hbm, lon_hbm,
     o_ref,
+    f_ref, lat_ref, lon_ref, in_sem, src_tiles,
     X, work, ca, cw, cd, acc, pacc,
     pack_l, pack_r,
     send_lb, send_rb, send_lc, send_rc, send_tb, send_bb, send_tc, send_bc,
@@ -62,6 +63,12 @@
         for lon_to in (me_lon, left, right):
             pl.semaphore_signal(barrier, 1, device_id={"lat": down, "lon": lon_to}, device_id_type=MESH)
 
+    loads = [pltpu.make_async_copy(f_hbm.at[i], f_ref.at[i], in_sem.at[i]) for i in range(slots)]
+    loads.append(pltpu.make_async_copy(lat_hbm, lat_ref, in_sem.at[slots]))
+    loads.append(pltpu.make_async_copy(lon_hbm, lon_ref, in_sem.at[slots + 1]))
+    for copy in loads:
+        copy.start()
+
     lane = lax.broadcasted_iota(jnp.int32, (height, 128), 1)
     quad = lane // HALO
     sub8 = lax.broadcasted_iota(jnp.int32, (STRIP, COLS), 0)
@@ -71,6 +78,11 @@
     zero_rows = jnp.zeros((TOP, COLS), jnp.float32)
 
     for a in range(count):
+        if a % fields == 0 and a < nfield:
+            loads[a // fields].wait()
+        if a == nfield:
+            loads[slots].wait()
+            loads[slots + 1].wait()
         if a < nfield:
             raw = f_ref[a // fields, a % fields].astype(jnp.float32)
         else:
@@ -200,6 +212,7 @@
 
     derive(8, rows - 16)
     acc[...] = jnp.zeros_like(acc)
+    src_tiles[:, :, 0] = jnp.zeros((2, steps, STRIP, COLS), jnp.float32)
 
     def slot_places(s):
         slot = member * slots + s
@@ -219,8 +232,10 @@
             cb = jnp.where(near, d, d - nlon_cells + COLS)
             valid = (rb >= TOP - HALO) & (rb < TOP + height + HALO) & (near | wrap)
             hit = (sub8 == lax.rem(jnp.maximum(rb, 0), 8)) & (lane_w == cb)
-            amps = [wav_ref[t] if comp == 0 else res_ref[steps - 1 - t, slot] for t in range(steps)]
-            places.append((rb, valid, hit, amps))
+            for t in range(steps):
+                amp = wav_ref[t] if comp == 0 else res_ref[steps - 1 - t, slot]
+                src_tiles[comp, t, 1] = jnp.where(hit, amp, jnp.float32(0.0))
+            places.append((rb, valid))
         return act, places
 
     def run_blocks(s, t, block_list, act, places):
@@ -235,8 +250,8 @@
             ww = cw[pl.ds(r0, 8), :]
             outs = []
             for comp in range(2):
-                rb, valid, hit, amps = places[comp]
-                amp = jnp.where(valid & (rb >= r0) & (rb < r0 + 8), amps[t], jnp.float32(0.0))
+                rb, valid = places[comp]
+                pick = (valid & (rb >= r0) & (rb < r0 + 8)).astype(jnp.int32)
                 cur_ref, ear_ref, nxt_ref = bufs[comp][ci], bufs[comp][ei], bufs[comp][ni]
                 cur = cur_ref[pl.ds(r0, 8), :]
                 above = cur_ref[pl.ds(r0 - 1, 8), :]
@@ -245,7 +260,7 @@
                 west = pltpu.roll(cur, 1, 1)
                 east = pltpu.roll(cur, COLS - 1, 1)
                 nxt = dd * cur + nn * below + aa * above + ee * east + ww * west - ear
-                nxt = nxt + jnp.where(hit, amp, jnp.float32(0.0))
+                nxt = nxt + src_tiles[comp, t, pick]
                 nxt_ref[pl.ds(r0, 8), :] = nxt
                 outs.append(nxt)
             if 2 <= k < blocks - 2:
@@ -345,9 +360,14 @@
     return pl.pallas_call(
         functools.partial(fused_kernel, nlon_cells),
         out_shape=jax.ShapeDtypeStruct((height, breadth), jnp.float32),
-        in_specs=[smem] * 5 + [vmem] * 3,
+        in_specs=[smem] * 5 + [pl.BlockSpec(memory_space=pl.ANY)] * 3,
         out_specs=vmem,
         scratch_shapes=[
+            pltpu.VMEM(wave_states.shape, wave_states.dtype),
+            pltpu.VMEM(lat_faces.shape, jnp.float32),
+            pltpu.VMEM(lon_faces.shape, jnp.float32),
+            pltpu.SemaphoreType.DMA((slots + 2,)),
+            pltpu.VMEM((2, 4, 2, STRIP, COLS), jnp.float32),
             pltpu.VMEM((count, rows, COLS), jnp.float32),
             pltpu.VMEM((slots, 2, rows, COLS), jnp.float32),
             plane,

time: 30.5 us -> 30.1 us (0.987)
  Pallas kernels: 28.6 us -> 28.2 us
    pallas_call x1, Pallas kernels: 28.6 us -> 28.2 us  [fused(): pl.pallas_call(functools.partial(fused_kernel, nlon_cells), out_shape=jax...]
where the time goes in v6:
time: 30.1 us; the launch traced here: 30 us
  Pallas kernels  28.2 us (94%)
  local copies, waits for them, and re-layouts  1.77 us (6%)
    pallas_call x1, Pallas kernels, fused(): pl.pallas_call(functools.partial(fused_kernel, nlon_cells), out_shape=jax...  28.2 us
    unnamed x1, local copies, waits for them, and re-layouts  1.77 us

profile of v6, /device:TPU:1, one launch (start us, length us, event | category | flops | bytes accessed | tf_op | source)
XLA Modules:
  0.0 30.0 jit_solution(1045874085279511187)
XLA Ops:
  0.0 28.2 %shard_map.82 = f32[192,448]{1,0:T(8,128)} custom-call(s32[2,8]{1,0:T(2,128)} %bitcast.3, s32[2]{0:T(128)} %pc_ref.1, f32[4,8]{1,0:T(4,128)} %bitcast.2, s32[256]{0:T(256)} %sc_ref.1, f32[4]{0:T(128)} %wav_ref.1, bf16[4,4,192,448]{3,2,1,0:T(8,128)(2,1)} %f_hbm.1, f32[192,448]{1,0:T(8,128)} %lat_hbm.1, f32[192,448]{1,0:T(8,128)} %lon_hbm.1), custom_call_target="tpu_custom_call" | custom-call | tf_op jit(solution)/shard_map/pallas_call | solution.py:360
  28.2 1.8 %copy.10 = f32[192,448]{1,0:T(8,128)} copy(f32[192,448]{1,0:T(8,128)} %shard_map.82) | data formatting | bytes 688128

commit v7 on v6

--- a/solution.py
+++ b/solution.py
@@ -13,6 +13,7 @@
 STRIP = 8
 MESH = pl.DeviceIdType.MESH
 TL, TR, BL, BR = 0, 1, 2, 3
+SPLIT = 80
 
 
 def fused_kernel(
@@ -21,7 +22,7 @@
     f_hbm, lat_hbm, lon_hbm,
     o_ref,
     f_ref, lat_ref, lon_ref, in_sem, src_tiles,
-    X, work, ca, cw, cd, acc, pacc,
+    X, work, ca, cw, cd, acc, pacc, SX, swork, sa, sw, sd, seam_src,
     pack_l, pack_r,
     send_lb, send_rb, send_lc, send_rc, send_tb, send_bb, send_tc, send_bc,
     rlb, rrb, rlc, rrc, rab, rbb, rac, rbc, rc,
@@ -140,6 +141,112 @@
             dst_b[j] = jnp.concatenate(both, axis=0).astype(jnp.bfloat16)
         dst_c[...] = strip_pair(nfield, first, keep_low)
 
+    def seam_of(t3, t0):
+        lane_x = lax.broadcasted_iota(jnp.int32, t3.shape, 1)
+        return jnp.where(lane_x < SPLIT, pltpu.roll(t3, SPLIT, 1), pltpu.roll(t0, SPLIT, 1))
+
+    for a in range(count):
+        SX[a] = seam_of(X[a, :, pl.ds(384, 128)], X[a, :, pl.ds(0, 128)])
+
+    def derive(first, size):
+        ca[pl.ds(first, size), :] = cn[pl.ds(first - 1, size), :]
+        cw[pl.ds(first, size), :] = pltpu.roll(ce[pl.ds(first, size), :], 1, 1)
+        cd[pl.ds(first, size), :] = 2.0 - (
+            cn[pl.ds(first, size), :] + ca[pl.ds(first, size), :] + ce[pl.ds(first, size), :] + cw[pl.ds(first, size), :]
+        )
+
+    derive(8, rows - 16)
+    acc[...] = jnp.zeros_like(acc)
+    src_tiles[:, :, 0] = jnp.zeros((2, steps, STRIP, COLS), jnp.float32)
+    seam_src[:, :, 0] = jnp.zeros((2, steps, STRIP, 128), jnp.float32)
+    lane_s8 = lax.broadcasted_iota(jnp.int32, (STRIP, 128), 1)
+    sub_s8 = lax.broadcasted_iota(jnp.int32, (STRIP, 128), 0)
+    keep = jnp.logical_not((lane_w < HALO) | ((lane_w >= breadth - HALO) & (lane_w < breadth)))
+
+    def slot_places(s, seam):
+        slot = member * slots + s
+        act = jnp.where(s < pc_ref[member], jnp.float32(1.0), jnp.float32(0.0))
+        row_first = me_lat * height
+        col_first = me_lon * breadth
+        places = []
+        for comp in range(2):
+            cell = sc_ref[pl_ref[comp, slot]]
+            r = lax.div(cell, nlon_cells)
+            c = cell - r * nlon_cells
+            rb = r - row_first + TOP
+            d = c - col_first
+            d = jnp.where(d < 0, d + nlon_cells, d)
+            near = d < breadth + HALO
+            wrap = d >= nlon_cells - HALO
+            cb = jnp.where(near, d, d - nlon_cells + COLS)
+            valid = (rb >= TOP - HALO) & (rb < TOP + height + HALO) & (near | wrap)
+            row8 = lax.rem(jnp.maximum(rb, 0), 8)
+            if seam:
+                in_seam = (cb >= 384 + 128 - SPLIT) | (cb < 128 - SPLIT)
+                valid = valid & in_seam
+                lane_at = jnp.where(cb >= 384 + 128 - SPLIT, cb - 384 - (128 - SPLIT), cb + SPLIT)
+                hit = (sub_s8 == row8) & (lane_s8 == lane_at)
+                tiles = seam_src
+            else:
+                hit = (sub8 == row8) & (lane_w == cb)
+                tiles = src_tiles
+            for t in range(steps):
+                amp = wav_ref[t] if comp == 0 else res_ref[steps - 1 - t, slot]
+                tiles[comp, t, 1] = jnp.where(hit, amp, jnp.float32(0.0))
+            places.append((rb, valid))
+        return act, places
+
+    def run_blocks(s, t, block_list, act, places, seam):
+        if seam:
+            bufs = [(SX.at[s * fields + comp], SX.at[s * fields + 2 + comp], swork.at[s, comp]) for comp in range(2)]
+            coefs = (sd, SX.at[nfield], sa, SX.at[nfield + 1], sw)
+            span, tiles = 128, seam_src
+        else:
+            bufs = [(X.at[s * fields + comp], X.at[s * fields + 2 + comp], work.at[s, comp]) for comp in range(2)]
+            coefs = (cd, cn, ca, ce, cw)
+            span, tiles = COLS, src_tiles
+        ei, ci, ni = t % 3, (t + 1) % 3, (t + 2) % 3
+        for k in block_list:
+            r0 = 8 * k
+            dd, nn, aa, ee, ww = (ref[pl.ds(r0, 8), :] for ref in coefs)
+            outs = []
+            for comp in range(2):
+                rb, valid = places[comp]
+                pick = (valid & (rb >= r0) & (rb < r0 + 8)).astype(jnp.int32)
+                cur_ref, ear_ref, nxt_ref = bufs[comp][ci], bufs[comp][ei], bufs[comp][ni]
+                cur = cur_ref[pl.ds(r0, 8), :]
+                above = cur_ref[pl.ds(r0 - 1, 8), :]
+                below = cur_ref[pl.ds(r0 + 1, 8), :]
+                ear = ear_ref[pl.ds(r0, 8), :]
+                west = pltpu.roll(cur, 1, 1)
+                east = pltpu.roll(cur, span - 1, 1)
+                nxt = dd * cur + nn * below + aa * above + ee * east + ww * west - ear
+                nxt = nxt + tiles[comp, t, pick]
+                nxt_ref[pl.ds(r0, 8), :] = nxt
+                outs.append(nxt)
+            if 2 <= k < blocks - 2:
+                prod = (outs[0] * act) * outs[1]
+                out_rows = pl.ds(r0 - TOP, 8)
+                if seam:
+                    back = pltpu.roll(prod, 128 - SPLIT, 1)
+                    acc[out_rows, pl.ds(0, 128)] += jnp.where(lane_s8 < HALO, back, jnp.float32(0.0))
+                    east_edge = (lane_s8 >= breadth - 384 - HALO) & (lane_s8 < breadth - 384)
+                    acc[out_rows, pl.ds(384, 128)] += jnp.where(east_edge, back, jnp.float32(0.0))
+                else:
+                    acc[out_rows, :] += jnp.where(keep, prod, jnp.float32(0.0))
+
+    def phase(ranges, seam=False):
+        def body(s, carry):
+            act, places = slot_places(s, seam)
+            for t in range(steps):
+                run_blocks(s, t, ranges(t), act, places, seam)
+            return carry
+
+        lax.fori_loop(0, slots, body, 0)
+
+    inner = lambda t: list(range(3 + t, blocks - 3 - t))
+    phase(inner)
+
     pl.semaphore_wait(barrier, 3 + 3 * has_up.astype(jnp.int32) + 3 * has_down.astype(jnp.int32))
 
     last8 = pl.ds(height - STRIP, STRIP)
@@ -180,8 +287,23 @@
     for i, copy in enumerate(copies):
         when(copy[4], lambda i=i: descriptor(i).start())
 
-    for i in range(4):
+    for i in range(len(copies)):
         finish(i)
+
+    @pl.when(jnp.logical_not(has_up))
+    def _():
+        rab[...] = jnp.zeros_like(rab)
+        rac[...] = jnp.zeros_like(rac)
+        rc[TL] = jnp.zeros((STRIP, 128), jnp.float32)
+        rc[TR] = jnp.zeros((STRIP, 128), jnp.float32)
+
+    @pl.when(jnp.logical_not(has_down))
+    def _():
+        rbb[...] = jnp.zeros_like(rbb)
+        rbc[...] = jnp.zeros_like(rbc)
+        rc[BL] = jnp.zeros((STRIP, 128), jnp.float32)
+        rc[BR] = jnp.zeros((STRIP, 128), jnp.float32)
+
     east_gap = (lane >= breadth - 384) & (lane < breadth - 384 + HALO)
     west_gap = lane >= 128 - HALO
     unpacked = []
@@ -195,105 +317,15 @@
             parts.append(jnp.where(lane8 < coef_lane, blk_f, blk_c))
         unpacked.append(jnp.concatenate(parts, axis=0))
     from_l, from_r = unpacked
+    east_s = (lane >= breadth - 384 - (128 - SPLIT)) & (lane < breadth - 384 - (128 - SPLIT) + HALO)
+    west_s = (lane >= SPLIT - HALO) & (lane < SPLIT)
     for a in range(count):
-        east_shift = (breadth - 384 - HALO * a) % 128
-        west_shift = (128 - HALO - HALO * a) % 128
-        tail = X[a, pl.ds(TOP, height), pl.ds(384, 128)]
-        tail = jnp.where(east_gap, pltpu.roll(from_r, east_shift, 1), tail)
-        tail = jnp.where(west_gap, pltpu.roll(from_l, west_shift, 1), tail)
-        X[a, pl.ds(TOP, height), pl.ds(384, 128)] = tail
-
-    def derive(first, size):
-        ca[pl.ds(first, size), :] = cn[pl.ds(first - 1, size), :]
-        cw[pl.ds(first, size), :] = pltpu.roll(ce[pl.ds(first, size), :], 1, 1)
-        cd[pl.ds(first, size), :] = 2.0 - (
-            cn[pl.ds(first, size), :] + ca[pl.ds(first, size), :] + ce[pl.ds(first, size), :] + cw[pl.ds(first, size), :]
-        )
-
-    derive(8, rows - 16)
-    acc[...] = jnp.zeros_like(acc)
-    src_tiles[:, :, 0] = jnp.zeros((2, steps, STRIP, COLS), jnp.float32)
-
-    def slot_places(s):
-        slot = member * slots + s
-        act = jnp.where(s < pc_ref[member], jnp.float32(1.0), jnp.float32(0.0))
-        row_first = me_lat * height
-        col_first = me_lon * breadth
-        places = []
-        for comp in range(2):
-            cell = sc_ref[pl_ref[comp, slot]]
-            r = lax.div(cell, nlon_cells)
-            c = cell - r * nlon_cells
-            rb = r - row_first + TOP
-            d = c - col_first
-            d = jnp.where(d < 0, d + nlon_cells, d)
-            near = d < breadth + HALO
-            wrap = d >= nlon_cells - HALO
-            cb = jnp.where(near, d, d - nlon_cells + COLS)
-            valid = (rb >= TOP - HALO) & (rb < TOP + height + HALO) & (near | wrap)
-            hit = (sub8 == lax.rem(jnp.maximum(rb, 0), 8)) & (lane_w == cb)
-            for t in range(steps):
-                amp = wav_ref[t] if comp == 0 else res_ref[steps - 1 - t, slot]
-                src_tiles[comp, t, 1] = jnp.where(hit, amp, jnp.float32(0.0))
-            places.append((rb, valid))
-        return act, places
-
-    def run_blocks(s, t, block_list, act, places):
-        bufs = [(X.at[s * fields + comp], X.at[s * fields + 2 + comp], work.at[s, comp]) for comp in range(2)]
-        ei, ci, ni = t % 3, (t + 1) % 3, (t + 2) % 3
-        for k in block_list:
-            r0 = 8 * k
-            dd = cd[pl.ds(r0, 8), :]
-            nn = cn[pl.ds(r0, 8), :]
-            aa = ca[pl.ds(r0, 8), :]
-            ee = ce[pl.ds(r0, 8), :]
-            ww = cw[pl.ds(r0, 8), :]
-            outs = []
-            for comp in range(2):
-                rb, valid = places[comp]
-                pick = (valid & (rb >= r0) & (rb < r0 + 8)).astype(jnp.int32)
-                cur_ref, ear_ref, nxt_ref = bufs[comp][ci], bufs[comp][ei], bufs[comp][ni]
-                cur = cur_ref[pl.ds(r0, 8), :]
-                above = cur_ref[pl.ds(r0 - 1, 8), :]
-                below = cur_ref[pl.ds(r0 + 1, 8), :]
-                ear = ear_ref[pl.ds(r0, 8), :]
-                west = pltpu.roll(cur, 1, 1)
-                east = pltpu.roll(cur, COLS - 1, 1)
-                nxt = dd * cur + nn * below + aa * above + ee * east + ww * west - ear
-                nxt = nxt + src_tiles[comp, t, pick]
-                nxt_ref[pl.ds(r0, 8), :] = nxt
-                outs.append(nxt)
-            if 2 <= k < blocks - 2:
-                acc[pl.ds(r0 - TOP, 8), :] += (outs[0] * act) * outs[1]
-
-    def phase(ranges):
-        def body(s, carry):
-            act, places = slot_places(s)
-            for t in range(steps):
-                run_blocks(s, t, ranges(t), act, places)
-            return carry
-
-        lax.fori_loop(0, slots, body, 0)
-
-    inner = lambda t: list(range(3 + t, blocks - 3 - t))
-    phase(inner)
-
-    for i in range(4, len(copies)):
-        finish(i)
-
-    @pl.when(jnp.logical_not(has_up))
-    def _():
-        rab[...] = jnp.zeros_like(rab)
-        rac[...] = jnp.zeros_like(rac)
-        rc[TL] = jnp.zeros((STRIP, 128), jnp.float32)
-        rc[TR] = jnp.zeros((STRIP, 128), jnp.float32)
-
-    @pl.when(jnp.logical_not(has_down))
-    def _():
-        rbb[...] = jnp.zeros_like(rbb)
-        rbc[...] = jnp.zeros_like(rbc)
-        rc[BL] = jnp.zeros((STRIP, 128), jnp.float32)
-        rc[BR] = jnp.zeros((STRIP, 128), jnp.float32)
+        east_shift = (breadth - 384 - (128 - SPLIT) - HALO * a) % 128
+        west_shift = (SPLIT - HALO - HALO * a) % 128
+        mid = SX[a, pl.ds(TOP, height), :]
+        mid = jnp.where(east_s, pltpu.roll(from_r, east_shift, 1), mid)
+        mid = jnp.where(west_s, pltpu.roll(from_l, west_shift, 1), mid)
+        SX[a, pl.ds(TOP, height), :] = mid
 
     east_c = (lane8 >= breadth - 384) & (lane8 < breadth - 384 + HALO)
     west_c = lane8 >= 128 - HALO
@@ -324,9 +356,17 @@
             tail = jnp.where(band & east_c, pltpu.roll(rc[c_east], east_shift, 1), tail)
             tail = jnp.where(band & west_c, pltpu.roll(rc[c_west], west_shift, 1), tail)
             X[a, pl.ds(first, STRIP), pl.ds(384, 128)] = tail
+            SX[a, pl.ds(first, STRIP), :] = seam_of(tail, blk[:, 0:128])
 
     derive(8, 24)
     derive(rows - 32, 24)
+    sn = SX.at[nfield]
+    se = SX.at[nfield + 1]
+    sa[pl.ds(8, rows - 16), :] = sn[pl.ds(7, rows - 16), :]
+    sw[pl.ds(8, rows - 16), :] = pltpu.roll(se[pl.ds(8, rows - 16), :], 1, 1)
+    sd[pl.ds(8, rows - 16), :] = 2.0 - (
+        sn[pl.ds(8, rows - 16), :] + sa[pl.ds(8, rows - 16), :] + se[pl.ds(8, rows - 16), :] + sw[pl.ds(8, rows - 16), :]
+    )
 
     def outer(t):
         if t < steps - 1:
@@ -334,6 +374,11 @@
         return list(range(2, 3 + t)) + list(range(blocks - 3 - t, blocks - 2))
 
     phase(outer)
+
+    def full(t):
+        return list(range(1, blocks - 1)) if t < steps - 1 else list(range(2, blocks - 2))
+
+    phase(full, seam=True)
 
     to_partner = pltpu.make_async_remote_copy(
         acc, pacc, send_sem.at[len(copies)], recv_sem.at[len(copies)], device_id={"pair": partner}, device_id_type=MESH
@@ -375,6 +420,12 @@
             plane,
             pltpu.VMEM((height, COLS), jnp.float32),
             pltpu.VMEM((height, COLS), jnp.float32),
+            pltpu.VMEM((count, rows, 128), jnp.float32),
+            pltpu.VMEM((slots, 2, rows, 128), jnp.float32),
+            pltpu.VMEM((rows, 128), jnp.float32),
+            pltpu.VMEM((rows, 128), jnp.float32),
+            pltpu.VMEM((rows, 128), jnp.float32),
+            pltpu.VMEM((2, 4, 2, STRIP, 128), jnp.float32),
             pltpu.VMEM((height, 128), jnp.float32),
             pltpu.VMEM((height, 128), jnp.float32),
         ]

time: 30.1 us -> 39 us (1.30)
  Pallas kernels: 28.2 us -> 37.1 us
    pallas_call x1, Pallas kernels: 28.2 us -> 37.1 us  [fused(): pl.pallas_call(functools.partial(fused_kernel, nlon_cells), out_shape=jax...]
where the time goes in v7:
time: 39 us; the launch traced here: 38.9 us
  Pallas kernels  37.1 us (95%)
  local copies, waits for them, and re-layouts  1.77 us (5%)
    pallas_call x1, Pallas kernels, fused(): pl.pallas_call(functools.partial(fused_kernel, nlon_cells), out_shape=jax...  37.1 us
    unnamed x1, local copies, waits for them, and re-layouts  1.77 us

profile of v7, /device:TPU:1, one launch (start us, length us, event | category | flops | bytes accessed | tf_op | source)
XLA Modules:
  0.0 38.9 jit_solution(745054299543113858)
XLA Ops:
  0.0 37.1 %shard_map.82 = f32[192,448]{1,0:T(8,128)} custom-call(s32[2,8]{1,0:T(2,128)} %bitcast.3, s32[2]{0:T(128)} %pc_ref.1, f32[4,8]{1,0:T(4,128)} %bitcast.2, s32[256]{0:T(256)} %sc_ref.1, f32[4]{0:T(128)} %wav_ref.1, bf16[4,4,192,448]{3,2,1,0:T(8,128)(2,1)} %f_hbm.1, f32[192,448]{1,0:T(8,128)} %lat_hbm.1, f32[192,448]{1,0:T(8,128)} %lon_hbm.1), custom_call_target="tpu_custom_call" | custom-call | tf_op jit(solution)/shard_map/pallas_call | solution.py:405
  37.1 1.8 %copy.10 = f32[192,448]{1,0:T(8,128)} copy(f32[192,448]{1,0:T(8,128)} %shard_map.82) | data formatting | bytes 688128

commit v8 on v6

--- a/solution.py
+++ b/solution.py
@@ -13,6 +13,7 @@
 STRIP = 8
 MESH = pl.DeviceIdType.MESH
 TL, TR, BL, BR = 0, 1, 2, 3
+MID_FIRST = 32
 
 
 def fused_kernel(
@@ -21,7 +22,7 @@
     f_hbm, lat_hbm, lon_hbm,
     o_ref,
     f_ref, lat_ref, lon_ref, in_sem, src_tiles,
-    X, work, ca, cw, cd, acc, pacc,
+    X, work, ca, cw, cd, acc, pacc, acc_mid, pacc_mid,
     pack_l, pack_r,
     send_lb, send_rb, send_lc, send_rc, send_tb, send_bb, send_tc, send_bc,
     rlb, rrb, rlc, rrc, rab, rbb, rac, rbc, rc,
@@ -212,6 +213,7 @@
 
     derive(8, rows - 16)
     acc[...] = jnp.zeros_like(acc)
+    acc_mid[...] = jnp.zeros_like(acc_mid)
     src_tiles[:, :, 0] = jnp.zeros((2, steps, STRIP, COLS), jnp.float32)
 
     def slot_places(s):
@@ -264,7 +266,12 @@
                 nxt_ref[pl.ds(r0, 8), :] = nxt
                 outs.append(nxt)
             if 2 <= k < blocks - 2:
-                acc[pl.ds(r0 - TOP, 8), :] += (outs[0] * act) * outs[1]
+                row = r0 - TOP
+                if MID_FIRST <= row < MID_FIRST + acc_mid.shape[0]:
+                    dst, row = acc_mid, row - MID_FIRST
+                else:
+                    dst, row = acc, (row if row < MID_FIRST else row - acc_mid.shape[0])
+                dst[pl.ds(row, 8), :] += (outs[0] * act) * outs[1]
 
     def phase(ranges):
         def body(s, carry):
@@ -277,6 +284,12 @@
 
     inner = lambda t: list(range(3 + t, blocks - 3 - t))
     phase(inner)
+
+    mid_out = pltpu.make_async_remote_copy(
+        acc_mid, pacc_mid, send_sem.at[len(copies) + 1], recv_sem.at[len(copies) + 1],
+        device_id={"pair": partner}, device_id_type=MESH,
+    )
+    mid_out.start()
 
     for i in range(4, len(copies)):
         finish(i)
@@ -340,7 +353,12 @@
     )
     to_partner.start()
     to_partner.wait()
-    o_ref[...] = (acc[...] + pacc[...])[:, 0:breadth]
+    mid_out.wait()
+    edge = acc[...] + pacc[...]
+    mids = acc_mid.shape[0]
+    o_ref[pl.ds(0, MID_FIRST), :] = edge[0:MID_FIRST, 0:breadth]
+    o_ref[pl.ds(MID_FIRST, mids), :] = (acc_mid[...] + pacc_mid[...])[:, 0:breadth]
+    o_ref[pl.ds(MID_FIRST + mids, height - MID_FIRST - mids), :] = edge[MID_FIRST:, 0:breadth]
 
 
 def fused(wave_states, lat_faces, lon_faces, scalars, nlon_cells):
@@ -373,16 +391,18 @@
             plane,
             plane,
             plane,
-            pltpu.VMEM((height, COLS), jnp.float32),
-            pltpu.VMEM((height, COLS), jnp.float32),
+            pltpu.VMEM((2 * MID_FIRST, COLS), jnp.float32),
+            pltpu.VMEM((2 * MID_FIRST, COLS), jnp.float32),
+            pltpu.VMEM((height - 2 * MID_FIRST, COLS), jnp.float32),
+            pltpu.VMEM((height - 2 * MID_FIRST, COLS), jnp.float32),
             pltpu.VMEM((height, 128), jnp.float32),
             pltpu.VMEM((height, 128), jnp.float32),
         ]
         + [packed_b, packed_b, packed_c, packed_c, strip_b16, strip_b16, strip_c, strip_c] * 2
         + [
             pltpu.VMEM((4, STRIP, 128), jnp.float32),
-            pltpu.SemaphoreType.DMA((13,)),
-            pltpu.SemaphoreType.DMA((13,)),
+            pltpu.SemaphoreType.DMA((14,)),
+            pltpu.SemaphoreType.DMA((14,)),
         ],
         compiler_params=pltpu.CompilerParams(collective_id=0, has_side_effects=True, vmem_limit_bytes=60 * 1024 * 1024),
     )(*scalars, wave_states, lat_faces, lon_faces)

time: 30.1 us -> 29.8 us (0.990)
  Pallas kernels: 28.2 us -> 27.8 us
    pallas_call x1, Pallas kernels: 28.2 us -> 27.8 us  [fused(): pl.pallas_call(functools.partial(fused_kernel, nlon_cells), out_shape=jax...]
where the time goes in v8:
time: 29.8 us; the launch traced here: 29.6 us
  Pallas kernels  27.8 us (93%)
  local copies, waits for them, and re-layouts  1.77 us (6%)
    pallas_call x1, Pallas kernels, fused(): pl.pallas_call(functools.partial(fused_kernel, nlon_cells), out_shape=jax...  27.8 us
    unnamed x1, local copies, waits for them, and re-layouts  1.77 us

profile of v8, /device:TPU:1, one launch (start us, length us, event | category | flops | bytes accessed | tf_op | source)
XLA Modules:
  0.0 29.6 jit_solution(7717845909148110882)
XLA Ops:
  0.0 27.8 %shard_map.82 = f32[192,448]{1,0:T(8,128)} custom-call(s32[2,8]{1,0:T(2,128)} %bitcast.3, s32[2]{0:T(128)} %pc_ref.1, f32[4,8]{1,0:T(4,128)} %bitcast.2, s32[256]{0:T(256)} %sc_ref.1, f32[4]{0:T(128)} %wav_ref.1, bf16[4,4,192,448]{3,2,1,0:T(8,128)(2,1)} %f_hbm.1, f32[192,448]{1,0:T(8,128)} %lat_hbm.1, f32[192,448]{1,0:T(8,128)} %lon_hbm.1), custom_call_target="tpu_custom_call" | custom-call | tf_op jit(solution)/shard_map/pallas_call | solution.py:378
  27.8 1.8 %copy.10 = f32[192,448]{1,0:T(8,128)} copy(f32[192,448]{1,0:T(8,128)} %shard_map.82) | data formatting | bytes 688128

commit v9 on v8

--- a/solution.py
+++ b/solution.py
@@ -354,11 +354,27 @@
     to_partner.start()
     to_partner.wait()
     mid_out.wait()
-    edge = acc[...] + pacc[...]
     mids = acc_mid.shape[0]
-    o_ref[pl.ds(0, MID_FIRST), :] = edge[0:MID_FIRST, 0:breadth]
-    o_ref[pl.ds(MID_FIRST, mids), :] = (acc_mid[...] + pacc_mid[...])[:, 0:breadth]
-    o_ref[pl.ds(MID_FIRST + mids, height - MID_FIRST - mids), :] = edge[MID_FIRST:, 0:breadth]
+    for side, (edge_ref, mid_ref) in enumerate(((acc, acc_mid), (pacc, pacc_mid))):
+        o_ref[side, pl.ds(0, MID_FIRST), :] = edge_ref[pl.ds(0, MID_FIRST), pl.ds(0, breadth)]
+        o_ref[side, pl.ds(MID_FIRST, mids), :] = mid_ref[:, pl.ds(0, breadth)]
+        o_ref[side, pl.ds(MID_FIRST + mids, height - MID_FIRST - mids), :] = edge_ref[
+            pl.ds(MID_FIRST, height - MID_FIRST - mids), pl.ds(0, breadth)
+        ]
+
+
+def add_kernel(parts_ref, o_ref):
+    o_ref[...] = parts_ref[0] + parts_ref[1]
+
+
+def add_parts(parts):
+    vmem = pl.BlockSpec(memory_space=pltpu.VMEM)
+    return pl.pallas_call(
+        add_kernel,
+        out_shape=jax.ShapeDtypeStruct(parts.shape[1:], parts.dtype),
+        in_specs=[vmem],
+        out_specs=vmem,
+    )(parts)
 
 
 def fused(wave_states, lat_faces, lon_faces, scalars, nlon_cells):
@@ -377,7 +393,7 @@
     plane = pltpu.VMEM((rows, COLS), jnp.float32)
     return pl.pallas_call(
         functools.partial(fused_kernel, nlon_cells),
-        out_shape=jax.ShapeDtypeStruct((height, breadth), jnp.float32),
+        out_shape=jax.ShapeDtypeStruct((2, height, breadth), jnp.float32),
         in_specs=[smem] * 5 + [pl.BlockSpec(memory_space=pl.ANY)] * 3,
         out_specs=vmem,
         scratch_shapes=[
@@ -421,7 +437,7 @@
     height, breadth = lat_faces.shape
     nlon_cells = breadth * lax.axis_size("lon")
     scalars = (pair_list.T, pair_counts, residuals.T, station_cell, source_wavelet)
-    return fused(wave_states, lat_faces, lon_faces, scalars, nlon_cells)
+    return add_parts(fused(wave_states, lat_faces, lon_faces, scalars, nlon_cells))
 
 
 def solution(mesh):

time: 29.8 us -> 30.1 us (1.010)
  Pallas kernels: 27.8 us -> 29.9 us
  local copies, waits for them, and re-layouts: 1.77 us -> 0 us
    pallas_call x0 -> x1, Pallas kernels: none -> 1.92 us  [add_parts(): pl.pallas_call(add_kernel, out_shape=jax.ShapeDtypeStruct(parts.shape[1:]...]
    unnamed x1 -> x0, local copies, waits for them, and re-layouts: 1.77 us -> none
where the time goes in v9:
time: 30.1 us; the launch traced here: 29.9 us
  Pallas kernels  29.9 us (99%)
    pallas_call x1, Pallas kernels, fused(): pl.pallas_call(functools.partial(fused_kernel, nlon_cells), out_shape=jax...  28 us
    pallas_call x1, Pallas kernels, add_parts(): pl.pallas_call(add_kernel, out_shape=jax.ShapeDtypeStruct(parts.shape[1:]...  1.92 us

profile of v9, /device:TPU:1, one launch (start us, length us, event | category | flops | bytes accessed | tf_op | source)
XLA Modules:
  0.0 29.9 jit_solution(5546476610185163953)
XLA Ops:
  0.0 28.0 %shard_map.82.parts_ref = f32[2,192,448]{2,1,0:T(8,128)} custom-call(s32[2,8]{1,0:T(2,128)} %bitcast.3, s32[2]{0:T(128)} %pc_ref.1, f32[4,8]{1,0:T(4,128)} %bitcast.2, s32[256]{0:T(256)} %sc_ref.1, f32[4]{0:T(128)} %wav_ref.1, bf16[4,4,192,448]{3,2,1,0:T(8,128)(2,1)} %f_hbm.1, f32[192,448]{1,0:T(8,128)} %lat_hbm.1, f32[192,448]{1,0:T(8,128)} %lon_hbm.1), custom_call_target="tpu_custom_call" | custom-call | tf_op jit(solution)/shard_map/pallas_call | solution.py:394
  28.0 1.9 %shard_map.83 = f32[192,448]{1,0:T(8,128)} custom-call(f32[2,192,448]{2,1,0:T(8,128)} %shard_map.82.parts_ref), custom_call_target="tpu_custom_call" | custom-call | tf_op jit(solution)/shard_map/pallas_call | solution.py:372

commit v10 on v8

--- a/solution.py
+++ b/solution.py
@@ -86,6 +86,9 @@
             loads[slots + 1].wait()
         if a < nfield:
             raw = f_ref[a // fields, a % fields].astype(jnp.float32)
+            if a % 2 == 0:
+                live = a // fields < pc_ref[member]
+                raw = raw * jnp.where(live, jnp.float32(1.0), jnp.float32(0.0))
         else:
             raw = (lat_ref if a == nfield else lon_ref)[...]
         X[a, pl.ds(TOP, height), pl.ds(0, breadth)] = raw
@@ -235,7 +238,7 @@
             valid = (rb >= TOP - HALO) & (rb < TOP + height + HALO) & (near | wrap)
             hit = (sub8 == lax.rem(jnp.maximum(rb, 0), 8)) & (lane_w == cb)
             for t in range(steps):
-                amp = wav_ref[t] if comp == 0 else res_ref[steps - 1 - t, slot]
+                amp = wav_ref[t] * act if comp == 0 else res_ref[steps - 1 - t, slot]
                 src_tiles[comp, t, 1] = jnp.where(hit, amp, jnp.float32(0.0))
             places.append((rb, valid))
         return act, places
@@ -271,7 +274,7 @@
                     dst, row = acc_mid, row - MID_FIRST
                 else:
                     dst, row = acc, (row if row < MID_FIRST else row - acc_mid.shape[0])
-                dst[pl.ds(row, 8), :] += (outs[0] * act) * outs[1]
+                dst[pl.ds(row, 8), :] += outs[0] * outs[1]
 
     def phase(ranges):
         def body(s, carry):

time: 29.8 us -> 29.6 us (level)
  no operation moved by 1% of the time
where the time goes in v10:
time: 29.6 us; the launch traced here: 29.5 us
  Pallas kernels  27.7 us (94%)
  local copies, waits for them, and re-layouts  1.77 us (6%)
    pallas_call x1, Pallas kernels, fused(): pl.pallas_call(functools.partial(fused_kernel, nlon_cells), out_shape=jax...  27.7 us
    unnamed x1, local copies, waits for them, and re-layouts  1.77 us

profile of v10, /device:TPU:1, one launch (start us, length us, event | category | flops | bytes accessed | tf_op | source)
XLA Modules:
  0.0 29.5 jit_solution(6803717165990768399)
XLA Ops:
  0.0 27.7 %shard_map.82 = f32[192,448]{1,0:T(8,128)} custom-call(s32[2,8]{1,0:T(2,128)} %bitcast.3, s32[2]{0:T(128)} %pc_ref.1, f32[4,8]{1,0:T(4,128)} %bitcast.2, s32[256]{0:T(256)} %sc_ref.1, f32[4]{0:T(128)} %wav_ref.1, bf16[4,4,192,448]{3,2,1,0:T(8,128)(2,1)} %f_hbm.1, f32[192,448]{1,0:T(8,128)} %lat_hbm.1, f32[192,448]{1,0:T(8,128)} %lon_hbm.1), custom_call_target="tpu_custom_call" | custom-call | tf_op jit(solution)/shard_map/pallas_call | solution.py:381
  27.7 1.8 %copy.10 = f32[192,448]{1,0:T(8,128)} copy(f32[192,448]{1,0:T(8,128)} %shard_map.82) | data formatting | bytes 688128

commit v11 on v10

--- a/solution.py
+++ b/solution.py
@@ -115,8 +115,11 @@
     coef_lane = HALO * nfield
     width = 2 * HALO
     per_row = 128 // width
-    send_lb[...] = pl_acc.astype(jnp.bfloat16)
-    send_rb[...] = pr_acc.astype(jnp.bfloat16)
+    half = height // 2
+    lane_h = lax.broadcasted_iota(jnp.int32, (half, 128), 1)
+    for src, dst in ((pl_acc, send_lb), (pr_acc, send_rb)):
+        folded = jnp.where(lane_h < coef_lane, src[0:half], pltpu.roll(src[half:height], coef_lane, 1))
+        dst[...] = folded.astype(jnp.bfloat16)
     for src, dst in ((pl_acc, send_lc), (pr_acc, send_rc)):
         for h in range(dst.shape[0] // STRIP):
             packed = jnp.zeros((STRIP, 128), jnp.float32)
@@ -190,7 +193,8 @@
     west_gap = lane >= 128 - HALO
     unpacked = []
     for src_b, src_c in ((rlb, rlc), (rrb, rrc)):
-        fields_part = src_b[...].astype(jnp.float32)
+        folded = src_b[...].astype(jnp.float32)
+        fields_part = jnp.concatenate([folded, pltpu.roll(folded, 128 - coef_lane, 1)], axis=0)
         parts = []
         for i in range(height // STRIP):
             h, g = divmod(i, per_row)
@@ -373,7 +377,7 @@
     vmem = pl.BlockSpec(memory_space=pltpu.VMEM)
     per_row = 128 // (2 * HALO)
     coef_rows = STRIP * ((height // STRIP + per_row - 1) // per_row)
-    packed_b = pltpu.VMEM((height, 128), jnp.bfloat16)
+    packed_b = pltpu.VMEM((height // 2, 128), jnp.bfloat16)
     packed_c = pltpu.VMEM((coef_rows, 128), jnp.float32)
     strip_b16 = pltpu.VMEM((nfield // 4, 2 * STRIP, COLS), jnp.bfloat16)
     strip_c = pltpu.VMEM((STRIP, COLS), jnp.float32)

time: 29.6 us -> 29.5 us (level)
  no operation moved by 1% of the time
where the time goes in v11:
time: 29.5 us; the launch traced here: 29.3 us
  Pallas kernels  27.5 us (93%)
  local copies, waits for them, and re-layouts  1.77 us (6%)
    pallas_call x1, Pallas kernels, fused(): pl.pallas_call(functools.partial(fused_kernel, nlon_cells), out_shape=jax...  27.5 us
    unnamed x1, local copies, waits for them, and re-layouts  1.77 us

profile of v11, /device:TPU:1, one launch (start us, length us, event | category | flops | bytes accessed | tf_op | source)
XLA Modules:
  0.0 29.3 jit_solution(7371458972298199068)
XLA Ops:
  0.0 27.5 %shard_map.82 = f32[192,448]{1,0:T(8,128)} custom-call(s32[2,8]{1,0:T(2,128)} %bitcast.3, s32[2]{0:T(128)} %pc_ref.1, f32[4,8]{1,0:T(4,128)} %bitcast.2, s32[256]{0:T(256)} %sc_ref.1, f32[4]{0:T(128)} %wav_ref.1, bf16[4,4,192,448]{3,2,1,0:T(8,128)(2,1)} %f_hbm.1, f32[192,448]{1,0:T(8,128)} %lat_hbm.1, f32[192,448]{1,0:T(8,128)} %lon_hbm.1), custom_call_target="tpu_custom_call" | custom-call | tf_op jit(solution)/shard_map/pallas_call | solution.py:385
  27.5 1.8 %copy.10 = f32[192,448]{1,0:T(8,128)} copy(f32[192,448]{1,0:T(8,128)} %shard_map.82) | data formatting | bytes 688128

commit v12 on v11

--- a/solution.py
+++ b/solution.py
@@ -22,7 +22,7 @@
     f_hbm, lat_hbm, lon_hbm,
     o_ref,
     f_ref, lat_ref, lon_ref, in_sem, src_tiles,
-    X, work, ca, cw, cd, acc, pacc, acc_mid, pacc_mid,
+    X, work, ca, cw, cd, acc, pacc, acc_mid, pacc_mid, acc_bot, pacc_bot,
     pack_l, pack_r,
     send_lb, send_rb, send_lc, send_rc, send_tb, send_bb, send_tc, send_bc,
     rlb, rrb, rlc, rrc, rab, rbb, rac, rbc, rc,
@@ -220,6 +220,7 @@
 
     derive(8, rows - 16)
     acc[...] = jnp.zeros_like(acc)
+    acc_bot[...] = jnp.zeros_like(acc_bot)
     acc_mid[...] = jnp.zeros_like(acc_mid)
     src_tiles[:, :, 0] = jnp.zeros((2, steps, STRIP, COLS), jnp.float32)
 
@@ -277,7 +278,7 @@
                 if MID_FIRST <= row < MID_FIRST + acc_mid.shape[0]:
                     dst, row = acc_mid, row - MID_FIRST
                 else:
-                    dst, row = acc, (row if row < MID_FIRST else row - acc_mid.shape[0])
+                    dst, row = (acc, row) if row < MID_FIRST else (acc_bot, row - MID_FIRST - acc_mid.shape[0])
                 dst[pl.ds(row, 8), :] += outs[0] * outs[1]
 
     def phase(ranges):
@@ -348,24 +349,31 @@
     derive(8, 24)
     derive(rows - 32, 24)
 
-    def outer(t):
-        if t < steps - 1:
-            return list(range(1, 3 + t)) + list(range(blocks - 3 - t, blocks - 1))
-        return list(range(2, 3 + t)) + list(range(blocks - 3 - t, blocks - 2))
-
-    phase(outer)
-
-    to_partner = pltpu.make_async_remote_copy(
-        acc, pacc, send_sem.at[len(copies)], recv_sem.at[len(copies)], device_id={"pair": partner}, device_id_type=MESH
-    )
-    to_partner.start()
-    to_partner.wait()
+    def outer_top(t):
+        return list(range(1, 3 + t)) if t < steps - 1 else list(range(2, 3 + t))
+
+    def outer_bottom(t):
+        return list(range(blocks - 3 - t, blocks - 1)) if t < steps - 1 else list(range(blocks - 3 - t, blocks - 2))
+
+    def to_other(i, src, dst):
+        return pltpu.make_async_remote_copy(
+            src, dst, send_sem.at[len(copies) + i], recv_sem.at[len(copies) + i],
+            device_id={"pair": partner}, device_id_type=MESH,
+        )
+
+    phase(outer_top)
+    top_out = to_other(2, acc, pacc)
+    top_out.start()
+    phase(outer_bottom)
+    bottom_out = to_other(3, acc_bot, pacc_bot)
+    bottom_out.start()
+    top_out.wait()
+    bottom_out.wait()
     mid_out.wait()
-    edge = acc[...] + pacc[...]
     mids = acc_mid.shape[0]
-    o_ref[pl.ds(0, MID_FIRST), :] = edge[0:MID_FIRST, 0:breadth]
+    o_ref[pl.ds(0, MID_FIRST), :] = (acc[...] + pacc[...])[:, 0:breadth]
     o_ref[pl.ds(MID_FIRST, mids), :] = (acc_mid[...] + pacc_mid[...])[:, 0:breadth]
-    o_ref[pl.ds(MID_FIRST + mids, height - MID_FIRST - mids), :] = edge[MID_FIRST:, 0:breadth]
+    o_ref[pl.ds(MID_FIRST + mids, height - MID_FIRST - mids), :] = (acc_bot[...] + pacc_bot[...])[:, 0:breadth]
 
 
 def fused(wave_states, lat_faces, lon_faces, scalars, nlon_cells):
@@ -398,18 +406,20 @@
             plane,
             plane,
             plane,
-            pltpu.VMEM((2 * MID_FIRST, COLS), jnp.float32),
-            pltpu.VMEM((2 * MID_FIRST, COLS), jnp.float32),
+            pltpu.VMEM((MID_FIRST, COLS), jnp.float32),
+            pltpu.VMEM((MID_FIRST, COLS), jnp.float32),
             pltpu.VMEM((height - 2 * MID_FIRST, COLS), jnp.float32),
             pltpu.VMEM((height - 2 * MID_FIRST, COLS), jnp.float32),
+            pltpu.VMEM((MID_FIRST, COLS), jnp.float32),
+            pltpu.VMEM((MID_FIRST, COLS), jnp.float32),
             pltpu.VMEM((height, 128), jnp.float32),
             pltpu.VMEM((height, 128), jnp.float32),
         ]
         + [packed_b, packed_b, packed_c, packed_c, strip_b16, strip_b16, strip_c, strip_c] * 2
         + [
             pltpu.VMEM((4, STRIP, 128), jnp.float32),
-            pltpu.SemaphoreType.DMA((14,)),
-            pltpu.SemaphoreType.DMA((14,)),
+            pltpu.SemaphoreType.DMA((16,)),
+            pltpu.SemaphoreType.DMA((16,)),
         ],
         compiler_params=pltpu.CompilerParams(collective_id=0, has_side_effects=True, vmem_limit_bytes=60 * 1024 * 1024),
     )(*scalars, wave_states, lat_faces, lon_faces)

time: 29.5 us -> 29.8 us (1.010)
  Pallas kernels: 27.5 us -> 27.9 us
    pallas_call x1, Pallas kernels: 27.5 us -> 27.9 us  [fused(): pl.pallas_call(functools.partial(fused_kernel, nlon_cells), out_shape=jax...]
where the time goes in v12:
time: 29.8 us; the launch traced here: 29.7 us
  Pallas kernels  27.9 us (94%)
  local copies, waits for them, and re-layouts  1.77 us (6%)
    pallas_call x1, Pallas kernels, fused(): pl.pallas_call(functools.partial(fused_kernel, nlon_cells), out_shape=jax...  27.9 us
    unnamed x1, local copies, waits for them, and re-layouts  1.77 us

profile of v12, /device:TPU:1, one launch (start us, length us, event | category | flops | bytes accessed | tf_op | source)
XLA Modules:
  0.0 29.7 jit_solution(16142964121372303194)
XLA Ops:
  0.0 27.9 %shard_map.82 = f32[192,448]{1,0:T(8,128)} custom-call(s32[2,8]{1,0:T(2,128)} %bitcast.3, s32[2]{0:T(128)} %pc_ref.1, f32[4,8]{1,0:T(4,128)} %bitcast.2, s32[256]{0:T(256)} %sc_ref.1, f32[4]{0:T(128)} %wav_ref.1, bf16[4,4,192,448]{3,2,1,0:T(8,128)(2,1)} %f_hbm.1, f32[192,448]{1,0:T(8,128)} %lat_hbm.1, f32[192,448]{1,0:T(8,128)} %lon_hbm.1), custom_call_target="tpu_custom_call" | custom-call | tf_op jit(solution)/shard_map/pallas_call | solution.py:393
  27.9 1.8 %copy.10 = f32[192,448]{1,0:T(8,128)} copy(f32[192,448]{1,0:T(8,128)} %shard_map.82) | data formatting | bytes 688128

commit v13 on v11

--- a/solution.py
+++ b/solution.py
@@ -287,7 +287,7 @@
                 run_blocks(s, t, ranges(t), act, places)
             return carry
 
-        lax.fori_loop(0, slots, body, 0)
+        lax.fori_loop(0, slots, body, 0, unroll=True)
 
     inner = lambda t: list(range(3 + t, blocks - 3 - t))
     phase(inner)

time: 29.5 us -> 30.4 us (1.031)
  Pallas kernels: 27.5 us -> 28.5 us
    pallas_call x1, Pallas kernels: 27.5 us -> 28.5 us  [fused(): pl.pallas_call(functools.partial(fused_kernel, nlon_cells), out_shape=jax...]
where the time goes in v13:
time: 30.4 us; the launch traced here: 30.3 us
  Pallas kernels  28.5 us (94%)
  local copies, waits for them, and re-layouts  1.77 us (6%)
    pallas_call x1, Pallas kernels, fused(): pl.pallas_call(functools.partial(fused_kernel, nlon_cells), out_shape=jax...  28.5 us
    unnamed x1, local copies, waits for them, and re-layouts  1.77 us

profile of v13, /device:TPU:1, one launch (start us, length us, event | category | flops | bytes accessed | tf_op | source)
XLA Modules:
  0.0 30.3 jit_solution(14812781458912042749)
XLA Ops:
  0.0 28.5 %shard_map.82 = f32[192,448]{1,0:T(8,128)} custom-call(s32[2,8]{1,0:T(2,128)} %bitcast.3, s32[2]{0:T(128)} %pc_ref.1, f32[4,8]{1,0:T(4,128)} %bitcast.2, s32[256]{0:T(256)} %sc_ref.1, f32[4]{0:T(128)} %wav_ref.1, bf16[4,4,192,448]{3,2,1,0:T(8,128)(2,1)} %f_hbm.1, f32[192,448]{1,0:T(8,128)} %lat_hbm.1, f32[192,448]{1,0:T(8,128)} %lon_hbm.1), custom_call_target="tpu_custom_call" | custom-call | tf_op jit(solution)/shard_map/pallas_call | solution.py:385
  28.5 1.8 %copy.10 = f32[192,448]{1,0:T(8,128)} copy(f32[192,448]{1,0:T(8,128)} %shard_map.82) | data formatting | bytes 688128

commit v14 on v11

--- a/solution.py
+++ b/solution.py
@@ -147,6 +147,10 @@
             dst_b[j] = jnp.concatenate(both, axis=0).astype(jnp.bfloat16)
         dst_c[...] = strip_pair(nfield, first, keep_low)
 
+    acc[...] = jnp.zeros_like(acc)
+    acc_mid[...] = jnp.zeros_like(acc_mid)
+    src_tiles[:, :, 0] = jnp.zeros((2, steps, STRIP, COLS), jnp.float32)
+
     pl.semaphore_wait(barrier, 3 + 3 * has_up.astype(jnp.int32) + 3 * has_down.astype(jnp.int32))
 
     last8 = pl.ds(height - STRIP, STRIP)
@@ -219,9 +223,6 @@
         )
 
     derive(8, rows - 16)
-    acc[...] = jnp.zeros_like(acc)
-    acc_mid[...] = jnp.zeros_like(acc_mid)
-    src_tiles[:, :, 0] = jnp.zeros((2, steps, STRIP, COLS), jnp.float32)
 
     def slot_places(s):
         slot = member * slots + s

time: 29.5 us -> 29.5 us (level)
  no operation moved by 1% of the time
where the time goes in v14:
time: 29.5 us; the launch traced here: 29.3 us
  Pallas kernels  27.5 us (93%)
  local copies, waits for them, and re-layouts  1.77 us (6%)
    pallas_call x1, Pallas kernels, fused(): pl.pallas_call(functools.partial(fused_kernel, nlon_cells), out_shape=jax...  27.5 us
    unnamed x1, local copies, waits for them, and re-layouts  1.77 us

profile of v14, /device:TPU:1, one launch (start us, length us, event | category | flops | bytes accessed | tf_op | source)
XLA Modules:
  0.0 29.3 jit_solution(7565340060605157247)
XLA Ops:
  0.0 27.5 %shard_map.82 = f32[192,448]{1,0:T(8,128)} custom-call(s32[2,8]{1,0:T(2,128)} %bitcast.3, s32[2]{0:T(128)} %pc_ref.1, f32[4,8]{1,0:T(4,128)} %bitcast.2, s32[256]{0:T(256)} %sc_ref.1, f32[4]{0:T(128)} %wav_ref.1, bf16[4,4,192,448]{3,2,1,0:T(8,128)(2,1)} %f_hbm.1, f32[192,448]{1,0:T(8,128)} %lat_hbm.1, f32[192,448]{1,0:T(8,128)} %lon_hbm.1), custom_call_target="tpu_custom_call" | custom-call | tf_op jit(solution)/shard_map/pallas_call | solution.py:386
  27.5 1.8 %copy.10 = f32[192,448]{1,0:T(8,128)} copy(f32[192,448]{1,0:T(8,128)} %shard_map.82) | data formatting | bytes 688128

commit v15 on v14

--- a/solution.py
+++ b/solution.py
@@ -188,8 +188,8 @@
         mirror = {None: None, "up": "down", "down": "up"}[cond]
         when(mirror, lambda: descriptor(i).wait_recv())
 
-    for i, copy in enumerate(copies):
-        when(copy[4], lambda i=i: descriptor(i).start())
+    for i in list(range(4, len(copies))) + list(range(4)):
+        when(copies[i][4], lambda i=i: descriptor(i).start())
 
     for i in range(4):
         finish(i)

time: 29.5 us -> 30.2 us (1.024)
  the two profiles are of different devices: /device:TPU:1 before, /device:TPU:27 now
where the time goes in v15:
time: 30.2 us; the launch traced here: 30 us
  Pallas kernels  28.2 us (93%)
  local copies, waits for them, and re-layouts  1.77 us (6%)
    pallas_call x1, Pallas kernels, fused(): pl.pallas_call(functools.partial(fused_kernel, nlon_cells), out_shape=jax...  28.2 us
    unnamed x1, local copies, waits for them, and re-layouts  1.77 us

profile of v15, /device:TPU:27, one launch (start us, length us, event | category | flops | bytes accessed | tf_op | source)
XLA Modules:
  0.0 30.0 jit_solution(2776058961830162531)
XLA Ops:
  0.0 28.2 %shard_map.82 = f32[192,448]{1,0:T(8,128)} custom-call(s32[2,8]{1,0:T(2,128)} %bitcast.3, s32[2]{0:T(128)} %pc_ref.1, f32[4,8]{1,0:T(4,128)} %bitcast.2, s32[256]{0:T(256)} %sc_ref.1, f32[4]{0:T(128)} %wav_ref.1, bf16[4,4,192,448]{3,2,1,0:T(8,128)(2,1)} %f_hbm.1, f32[192,448]{1,0:T(8,128)} %lat_hbm.1, f32[192,448]{1,0:T(8,128)} %lon_hbm.1), custom_call_target="tpu_custom_call" | custom-call | tf_op jit(solution)/shard_map/pallas_call | solution.py:386
  28.2 1.8 %copy.10 = f32[192,448]{1,0:T(8,128)} copy(f32[192,448]{1,0:T(8,128)} %shard_map.82) | data formatting | bytes 688128
